TPU v7x, 32 devices: a whole 2x2x4 slice. The times are simulated.
32 devices in a mesh: seq: 4 (over y, x), fsdp: 8 (over z, core).
Axes of the slice: x: 2, y: 2, z: 4, core: 2. Of those that a mesh axis runs over, the one named last changes fastest.
Arguments:
- tokens: bfloat16 [8, 1536, 1024], P('fsdp', 'seq'), may hold values from -6 to 6
- segment_ids: int32 [8, 1536], P('fsdp', 'seq'), may hold values from 0 to 5, never falling along the last dimension, each value on 1 to 768 neighbouring positions
- random_blocks: int32 [16, 22, 3], P('seq'), may hold values from 1 to 22, as said below
- ln1_gain: bfloat16 [1024], P('fsdp'), may hold values from 0.099609375 to 1.8984375
- ln1_bias: bfloat16 [1024], P('fsdp'), may hold values from -4 to 4
- w_qkv: bfloat16 [1024, 3072], P('fsdp'), may hold values from -0.25 to 0.25
- w_out: bfloat16 [1024, 1024], P('fsdp'), may hold values from -0.5 to 0.5
- ln2_gain: bfloat16 [1024], P('fsdp'), may hold values from 0.099609375 to 1.8984375
- ln2_bias: bfloat16 [1024], P('fsdp'), may hold values from -4 to 4
- w_in: bfloat16 [1024, 4096], P('fsdp'), may hold values from -0.1875 to 0.1875
- b_in: bfloat16 [4096], P('fsdp'), may hold values from -4 to 4
- w_down: bfloat16 [4096, 1024], P('fsdp'), may hold values from -0.09375 to 0.09375
- b_down: bfloat16 [1024], P('fsdp'), may hold values from -4 to 4
- cotangent: bfloat16 [8, 1536, 1024], P('fsdp', 'seq'), may hold values from -6 to 6
Outputs:
- output: bfloat16 [8, 1536, 1024], P('fsdp', 'seq')
- grad_tokens: bfloat16 [8, 1536, 1024], P('fsdp', 'seq')
- grad_ln1_gain: float32 [1024], P('fsdp')
- grad_ln1_bias: float32 [1024], P('fsdp')
- grad_qkv: float32 [1024, 3072], P('fsdp')
- grad_out_proj: float32 [1024, 1024], P('fsdp')
- grad_ln2_gain: float32 [1024], P('fsdp')
- grad_ln2_bias: float32 [1024], P('fsdp')
- grad_in: float32 [1024, 4096], P('fsdp')
- grad_in_bias: float32 [4096], P('fsdp')
- grad_down: float32 [4096, 1024], P('fsdp')
- grad_down_bias: float32 [1024], P('fsdp')
Inputs may be any that keep to these rules, and one draw needn't show every extreme that they name: For head h and query block b + 1, the 3 entries random_blocks[h, b, :] are different key blocks, none of them 0, 23, b, b + 1 or b + 2. `segment_ids`: in each sequence the segment numbers start at 0, never fall and take every value up to 5; a document has at most 768 tokens, and some document has exactly that many.
All inputs are finite; a program needn't handle non-finite values.
Results may differ from a plain program's by a relative error of at most 0.014.
Values may be sent and summed in bfloat16 or wider, within the bound.
A program may use at most 256 MiB of HBM per device.

v0:
```python
import math

import jax
import jax.numpy as jnp
from jax import lax
from jax.sharding import PartitionSpec as P

DH = 64
BLK = 64


def build_lists(random_blocks, blocks):
    middle_ids = jnp.arange(1, blocks - 1, dtype=jnp.int32)
    head_count = random_blocks.shape[0]
    window_ids = jnp.stack([middle_ids - 1, middle_ids, middle_ids + 1], axis=-1)
    global_ids = jnp.stack(
        [jnp.zeros_like(middle_ids), jnp.full_like(middle_ids, blocks - 1)], axis=-1
    )
    block_list = jnp.concatenate(
        [
            jnp.broadcast_to(window_ids, (head_count, blocks - 2, 3)),
            random_blocks,
            jnp.broadcast_to(global_ids, (head_count, blocks - 2, 2)),
        ],
        axis=-1,
    )
    usable = jnp.concatenate(
        [
            jnp.ones((blocks - 2, 3 + random_blocks.shape[2]), dtype=bool),
            (middle_ids != 1)[:, None],
            (middle_ids != blocks - 2)[:, None],
        ],
        axis=-1,
    )
    return (block_list, usable)


def masked_softmax(scores, allowed):
    shifted = jnp.where(allowed, scores, -1e30)
    top_score = jnp.max(shifted, axis=-1, keepdims=True)
    log_total = top_score + jnp.log(jnp.sum(jnp.exp(shifted - top_score), axis=-1, keepdims=True))
    return (jnp.exp(shifted - log_total), log_total)


def layer_norm(token_rows, gain_vec, bias_vec):
    center = token_rows - jnp.mean(token_rows, axis=-1, keepdims=True)
    variance = jnp.mean(center * center, axis=-1, keepdims=True)
    return center * lax.rsqrt(variance + 1e-05) * gain_vec + bias_vec


def gelu_tanh(pre_act):
    return (
        0.5
        * pre_act
        * (1.0 + jnp.tanh(0.7978845608028654 * (pre_act + 0.044715 * pre_act * pre_act * pre_act)))
    )


def lead_dot(left_arr, right_arr):
    return lax.dot_general(
        left_arr, right_arr, (((0,), (0,)), ((), ())), preferred_element_type=jnp.float32
    )


def last_dot(left_arr, right_arr):
    return lax.dot_general(
        left_arr, right_arr, (((1,), (1,)), ((), ())), preferred_element_type=jnp.float32
    )


def head_setup(queries, keys_all, values_all, block_list, usable, segments):
    length = queries.shape[0]
    blocks = length // BLK
    slot_count = block_list.shape[1]
    blocked_queries = queries.reshape(blocks, BLK, DH)
    neighbour_keys = keys_all.reshape(blocks, BLK, DH)[block_list].reshape(
        blocks - 2, slot_count * BLK, DH
    )
    neighbour_values = values_all.reshape(blocks, BLK, DH)[block_list].reshape(
        blocks - 2, slot_count * BLK, DH
    )
    seg_blocks = segments.reshape(blocks, BLK)
    key_seg = seg_blocks[block_list].reshape(blocks - 2, slot_count * BLK)
    allowed = (seg_blocks[1:-1][:, :, None] == key_seg[:, None, :]) & jnp.repeat(
        usable, BLK, axis=1
    )[:, None, :]
    edge_queries = jnp.concatenate([blocked_queries[0], blocked_queries[-1]], axis=0)
    edge_seg = jnp.concatenate([seg_blocks[0], seg_blocks[-1]], axis=0)
    edge_allowed = edge_seg[:, None] == segments[None, :]
    return (blocked_queries, neighbour_keys, neighbour_values, allowed, edge_queries, edge_allowed)


def head_forward(queries, keys_all, values_all, block_list, usable, segments):
    score_scale = 1.0 / math.sqrt(DH)
    blocked_queries, neighbour_keys, neighbour_values, allowed, edge_queries, edge_allowed = (
        head_setup(queries, keys_all, values_all, block_list, usable, segments)
    )
    unscaled_scores = jnp.einsum(
        "vfn,vmn->vfm", blocked_queries[1:-1], neighbour_keys, preferred_element_type=jnp.float32
    )
    middle_probability, log_mid = masked_softmax(unscaled_scores * score_scale, allowed)
    middle_output = jnp.einsum(
        "icf,ifl->icl",
        middle_probability.astype(jnp.bfloat16),
        neighbour_values,
        preferred_element_type=jnp.float32,
    )
    edge_raw = last_dot(edge_queries, keys_all)
    prob_edge, log_edge = masked_softmax(edge_raw * score_scale, edge_allowed)
    out_edge = jnp.dot(
        prob_edge.astype(jnp.bfloat16), values_all, preferred_element_type=jnp.float32
    )
    merged = jnp.concatenate(
        [out_edge[:BLK], middle_output.reshape(-1, DH), out_edge[BLK:]], axis=0
    )
    return (merged, log_mid, log_edge)


def head_backward(
    queries, keys_all, values_all, block_list, log_mid, log_edge, grad_out, usable, segments
):
    score_scale = 1.0 / math.sqrt(DH)
    length = queries.shape[0]
    blocks = length // BLK
    slot_count = block_list.shape[1]
    blocked_queries, neighbour_keys, neighbour_values, allowed, edge_queries, edge_allowed = (
        head_setup(queries, keys_all, values_all, block_list, usable, segments)
    )
    unscaled_scores = jnp.einsum(
        "vfn,vmn->vfm", blocked_queries[1:-1], neighbour_keys, preferred_element_type=jnp.float32
    )
    middle_probability = jnp.exp(jnp.where(allowed, unscaled_scores * score_scale, -1e30) - log_mid)
    middle_lower_precision = middle_probability.astype(jnp.bfloat16)
    grad_blocks = grad_out.reshape(blocks, BLK, DH)
    middle_block_gradient = grad_blocks[1:-1]
    grad_prob = jnp.einsum(
        "vfn,vmn->vfm", middle_block_gradient, neighbour_values, preferred_element_type=jnp.float32
    )
    delta_mid = jnp.sum(grad_prob * middle_probability, axis=-1, keepdims=True)
    score_gradient = (middle_probability * (grad_prob - delta_mid) * score_scale).astype(
        jnp.bfloat16
    )
    grad_query_mid = jnp.einsum(
        "icf,ifl->icl", score_gradient, neighbour_keys, preferred_element_type=jnp.float32
    )
    near_shape = (blocks - 2, slot_count, BLK, DH)
    grad_near_keys = jnp.einsum(
        "onm,ons->oms", score_gradient, blocked_queries[1:-1], preferred_element_type=jnp.float32
    ).reshape(near_shape)
    grad_near_values = jnp.einsum(
        "onm,ons->oms",
        middle_lower_precision,
        middle_block_gradient,
        preferred_element_type=jnp.float32,
    ).reshape(near_shape)
    edge_raw = last_dot(edge_queries, keys_all)
    prob_edge = jnp.exp(jnp.where(edge_allowed, edge_raw * score_scale, -1e30) - log_edge)
    edge_low = prob_edge.astype(jnp.bfloat16)
    grad_edge = jnp.concatenate([grad_blocks[0], grad_blocks[-1]], axis=0)
    grad_edge_prob = last_dot(grad_edge, values_all)
    delta_edge = jnp.sum(grad_edge_prob * prob_edge, axis=-1, keepdims=True)
    grad_edge_scores = (prob_edge * (grad_edge_prob - delta_edge) * score_scale).astype(
        jnp.bfloat16
    )
    grad_query_edge = jnp.dot(grad_edge_scores, keys_all, preferred_element_type=jnp.float32)
    grad_keys = (
        lead_dot(grad_edge_scores, edge_queries)
        .reshape(blocks, BLK, DH)
        .at[block_list]
        .add(grad_near_keys)
    )
    grad_values = (
        lead_dot(edge_low, grad_edge).reshape(blocks, BLK, DH).at[block_list].add(grad_near_values)
    )
    grad_queries = jnp.concatenate(
        [grad_query_edge[:BLK], grad_query_mid.reshape(-1, DH), grad_query_edge[BLK:]], axis=0
    )
    return jnp.stack(
        [grad_queries, grad_keys.reshape(-1, DH), grad_values.reshape(-1, DH)], axis=0
    ).astype(jnp.bfloat16)


def per_device(
    tokens,
    segment_ids,
    random_blocks,
    ln1_gain,
    ln1_bias,
    w_qkv,
    w_out,
    ln2_gain,
    ln2_bias,
    w_in,
    b_in,
    w_down,
    b_down,
    cotangent,
):
    gain_one, bias_one, qkv_weight, out_weight = (
        lax.all_gather(ln1_gain, "fsdp", axis=0, tiled=True),
        lax.all_gather(ln1_bias, "fsdp", axis=0, tiled=True),
        lax.all_gather(w_qkv, "fsdp", axis=0, tiled=True),
        lax.all_gather(w_out, "fsdp", axis=0, tiled=True),
    )
    gain_two, bias_two, in_weight, in_bias, down_weight, down_bias = (
        lax.all_gather(ln2_gain, "fsdp", axis=0, tiled=True),
        lax.all_gather(ln2_bias, "fsdp", axis=0, tiled=True),
        lax.all_gather(w_in, "fsdp", axis=0, tiled=True),
        lax.all_gather(b_in, "fsdp", axis=0, tiled=True),
        lax.all_gather(w_down, "fsdp", axis=0, tiled=True),
        lax.all_gather(b_down, "fsdp", axis=0, tiled=True),
    )
    token_rows = tokens[0].astype(jnp.float32)
    tok_count, width = token_rows.shape
    norm_one, pull_one = jax.vjp(
        layer_norm, token_rows, gain_one.astype(jnp.float32), bias_one.astype(jnp.float32)
    )
    normed_one = norm_one.astype(jnp.bfloat16)
    qkv_rows = (
        jnp.dot(normed_one, qkv_weight, preferred_element_type=jnp.float32)
        .astype(jnp.bfloat16)
        .reshape(tok_count, 3, width)
    )
    by_heads = lax.all_to_all(qkv_rows, "seq", split_axis=2, concat_axis=0, tiled=True)
    seq_ids = lax.all_gather(segment_ids[0], "seq", axis=0, tiled=True)
    length = by_heads.shape[0]
    head_count = random_blocks.shape[0]
    head_split = by_heads.reshape(length, 3, head_count, DH).transpose(1, 2, 0, 3)
    block_list, usable = build_lists(random_blocks, length // BLK)

    def forward_head(operands):
        return head_forward(operands[0], operands[1], operands[2], operands[3], usable, seq_ids)

    head_out, log_mid, log_edge = lax.map(
        forward_head, (head_split[0], head_split[1], head_split[2], block_list)
    )
    att_heads = head_out.transpose(1, 0, 2).reshape(length, head_count * DH).astype(jnp.bfloat16)
    att_rows = lax.all_to_all(att_heads, "seq", split_axis=0, concat_axis=1, tiled=True)
    branch = jnp.dot(att_rows, out_weight, preferred_element_type=jnp.float32)
    hidden = token_rows + branch
    norm_two, pull_two = jax.vjp(
        layer_norm, hidden, gain_two.astype(jnp.float32), bias_two.astype(jnp.float32)
    )
    normed_two = norm_two.astype(jnp.bfloat16)
    pre_act = jnp.dot(normed_two, in_weight, preferred_element_type=jnp.float32) + in_bias.astype(
        jnp.float32
    )
    act_value, pull_gelu = jax.vjp(gelu_tanh, pre_act)
    act_low = act_value.astype(jnp.bfloat16)
    result = (
        hidden
        + jnp.dot(act_low, down_weight, preferred_element_type=jnp.float32)
        + down_bias.astype(jnp.float32)
    )
    cot_low = cotangent[0]
    cot_rows = cot_low.astype(jnp.float32)
    in_back, down_back = (
        lax.all_gather(w_in, "fsdp", axis=0, tiled=True),
        lax.all_gather(w_down, "fsdp", axis=0, tiled=True),
    )
    grad_down = lead_dot(act_low, cot_low)
    grad_down_bias = jnp.sum(cot_rows, axis=0)
    grad_act = last_dot(cot_low, down_back)
    grad_pre = pull_gelu(grad_act)[0].astype(jnp.bfloat16)
    grad_in = lead_dot(normed_two, grad_pre)
    grad_in_bias = jnp.sum(grad_pre.astype(jnp.float32), axis=0)
    grad_norm_two = last_dot(grad_pre, in_back)
    grad_hidden_norm, grad_gain_two, grad_bias_two = pull_two(grad_norm_two)
    grad_hidden = cot_rows + grad_hidden_norm
    ffn_shares = (
        lax.psum_scatter(grad_gain_two, "fsdp", scatter_dimension=0, tiled=True),
        lax.psum_scatter(grad_bias_two, "fsdp", scatter_dimension=0, tiled=True),
        lax.psum_scatter(grad_in, "fsdp", scatter_dimension=0, tiled=True),
        lax.psum_scatter(grad_in_bias, "fsdp", scatter_dimension=0, tiled=True),
        lax.psum_scatter(grad_down, "fsdp", scatter_dimension=0, tiled=True),
        lax.psum_scatter(grad_down_bias, "fsdp", scatter_dimension=0, tiled=True),
    )
    qkv_back, out_back = (
        lax.all_gather(w_qkv, "fsdp", axis=0, tiled=True),
        lax.all_gather(w_out, "fsdp", axis=0, tiled=True),
    )
    hidden_low = grad_hidden.astype(jnp.bfloat16)
    grad_out_proj = lead_dot(att_rows, hidden_low)
    grad_att = last_dot(hidden_low, out_back).astype(jnp.bfloat16)
    grad_att_heads = lax.all_to_all(grad_att, "seq", split_axis=1, concat_axis=0, tiled=True)
    grad_split = grad_att_heads.reshape(length, head_count, DH).transpose(1, 0, 2)

    def backward_head(operands):
        return head_backward(
            operands[0],
            operands[1],
            operands[2],
            operands[3],
            operands[4],
            operands[5],
            operands[6],
            usable,
            seq_ids,
        )

    head_grads = lax.map(
        backward_head,
        (head_split[0], head_split[1], head_split[2], block_list, log_mid, log_edge, grad_split),
    )
    grad_heads = head_grads.transpose(2, 1, 0, 3).reshape(length, 3, head_count * DH)
    grad_qkv_rows = lax.all_to_all(
        grad_heads, "seq", split_axis=0, concat_axis=2, tiled=True
    ).reshape(tok_count, 3 * width)
    grad_qkv = lead_dot(normed_one, grad_qkv_rows)
    grad_norm_one = last_dot(grad_qkv_rows, qkv_back)
    grad_rows_norm, grad_gain_one, grad_bias_one = pull_one(grad_norm_one)
    grad_tokens = (grad_hidden + grad_rows_norm).astype(jnp.bfloat16)[None]
    attn_shares = (
        lax.psum_scatter(grad_gain_one, "fsdp", scatter_dimension=0, tiled=True),
        lax.psum_scatter(grad_bias_one, "fsdp", scatter_dimension=0, tiled=True),
        lax.psum_scatter(grad_qkv, "fsdp", scatter_dimension=0, tiled=True),
        lax.psum_scatter(grad_out_proj, "fsdp", scatter_dimension=0, tiled=True),
    )
    shares = attn_shares + ffn_shares
    totals = lax.psum(
        (
            shares[0],
            shares[1],
            shares[2],
            shares[3],
            shares[4],
            shares[5],
            shares[6],
            shares[7],
            shares[8],
            shares[9],
        ),
        "seq",
    )
    return (
        result.astype(jnp.bfloat16)[None],
        grad_tokens,
        totals[0],
        totals[1],
        totals[2],
        totals[3],
        totals[4],
        totals[5],
        totals[6],
        totals[7],
        totals[8],
        totals[9],
    )


def solution(mesh):
    return jax.shard_map(
        per_device,
        mesh=mesh,
        in_specs=(
            P("fsdp", "seq", None),
            P("fsdp", "seq"),
            P("seq", None, None),
            P("fsdp"),
            P("fsdp"),
            P("fsdp", None),
            P("fsdp", None),
            P("fsdp"),
            P("fsdp"),
            P("fsdp", None),
            P("fsdp"),
            P("fsdp", None),
            P("fsdp"),
            P("fsdp", "seq", None),
        ),
        out_specs=(
            P("fsdp", "seq", None),
            P("fsdp", "seq", None),
            P("fsdp"),
            P("fsdp"),
            P("fsdp", None),
            P("fsdp", None),
            P("fsdp"),
            P("fsdp"),
            P("fsdp", None),
            P("fsdp"),
            P("fsdp", None),
            P("fsdp"),
        ),
        check_vma=False,
    )
```

profile of v0, /device:TPU:0, one launch (start us, length us, event | category | flops | bytes accessed | tf_op | source)
XLA Modules:
  0.0 1317.9 jit_solution(9193868924157783332)
XLA Ops:
  9.4 13.5 %all-gather.1 = bf16[8,1,128]{2,1,0:T(2,128)(2,1)S(1)} all-gather(bf16[1,1,128]{2,1,0:T(2,128)(2,1)} %bitcast.348), channel_id=1, replica_groups=mesh['seq'=4,'fsdp'=8] {'fsdp'}, dimensions={0}, use_global_device_ids=true | all-gather | bytes 2304 | tf_op jit(solution)/shard_map/all_gather | solution.py:200
  23.0 8.8 all-gather.2
  34.1 43.1 %all-gather.12.cloned.1.call-done = bf16[1024,3072]{1,0:T(8,128)(2,1)} async-done(((bf16[128,3072]{1,0:T(8,128)(2,1)}), bf16[1024,3072]{1,0:T(8,128)(2,1)}) %all-gather.12.cloned.1.call-update) | async-done | bytes 6291472 | tf_op jit(solution)/shard_map/all_gather | solution.py:202
  95.4 39.0 %all-gather = s32[1,1536]{1,0:T(1,128)S(1)} all-gather(s32[1,384]{1,0:T(1,128)S(1)} %copy-done.53), channel_id=2, replica_groups=mesh['seq'=4,'fsdp'=8] {'seq'}, dimensions={1}, use_global_device_ids=true | all-gather | bytes 7680 | tf_op jit(solution)/shard_map/all_gather | solution.py:225
  149.5 64.8 %while.26 = (s32[]{:T(128)}, bf16[4,1536,64]{2,1,0:T(8,128)(2,1)}, f32[4,22,64,1]{2,1,3,0:T(8,128)}, f32[4,128,1]{1,2,0:T(1,128)}, s32[128]{0:T(128)S(1)}, /*ind...) while((s32[]{:T(128)}, bf16[4,1536,64]{2,1,0:T(8,128)(2,1)}, ...), condition=%wide.region_7.8_spmd, body=%wide.region_2.7_spmd.sunk | while | flops 243564560 | bytes 28432796 | solution.py:234
  220.7 9.4 all-gather.3
  230.1 10.3 all-gather.4
  240.4 13.0 all-gather.5
  256.5 9.3 convolution_add_fusion
  272.0 11.9 convert_reduce_fusion
  309.4 333.9 %while.27 = (s32[]{:T(128)}, bf16[4,3,1536,64]{2,3,0,1:T(8,128)(2,1)}, s32[128]{0:T(128)S(1)}, s32[1536]{0:T(1024)S(1)}, bf16[4,1536,64]{2,1,0:T(8,128)(2,1)}, /...) while((s32[]{:T(128)}, ...), condition=%wide.region_17.18_spmd, body=%wide.region_12.17_spmd.sunk | while | flops 603952256 | bytes 75161568 | solution.py:301
  340.6 8.3 fusion.198
  348.9 18.4 %scatter_fusion.1 = f32[24,64,64]{2,1,0:T(8,128)S(1)} fusion(f32[24,64,64]{2,1,0:T(8,128)S(1)} %bitcast.297, s32[176]{0:T(256)S(1)} %reshape.627, f32[176,64,64]{2,1,0:T(8,128)} %bitcast.303), kind=kCustom, calls=%fused_computation.6.clone.1 | custom fusion | flops 720896 | bytes 8651456 | tf_op jit(solution)/shard_map/while/body/eval_jaxpr/scatter-add | solution.py:170
  372.7 18.4 %scatter_fusion = f32[24,64,64]{2,1,0:T(8,128)S(1)} fusion(f32[24,64,64]{2,1,0:T(8,128)S(1)} %bitcast.296, s32[176]{0:T(256)S(1)} %reshape.627, f32[176,64,64]{2,1,0:T(8,128)} %bitcast.302), kind=kCustom, calls=%fused_computation.7.clone.1 | custom fusion | flops 720896 | bytes 8651456 | tf_op jit(solution)/shard_map/while/body/eval_jaxpr/scatter-add | solution.py:173
  432.4 18.4 %scatter_fusion.1 = f32[24,64,64]{2,1,0:T(8,128)S(1)} fusion(f32[24,64,64]{2,1,0:T(8,128)S(1)} %bitcast.297, s32[176]{0:T(256)S(1)} %reshape.627, f32[176,64,64]{2,1,0:T(8,128)} %bitcast.303), kind=kCustom, calls=%fused_computation.6.clone.1 | custom fusion | flops 720896 | bytes 8651456 | tf_op jit(solution)/shard_map/while/body/eval_jaxpr/scatter-add | solution.py:170
  456.1 18.4 %scatter_fusion = f32[24,64,64]{2,1,0:T(8,128)S(1)} fusion(f32[24,64,64]{2,1,0:T(8,128)S(1)} %bitcast.296, s32[176]{0:T(256)S(1)} %reshape.627, f32[176,64,64]{2,1,0:T(8,128)} %bitcast.302), kind=kCustom, calls=%fused_computation.7.clone.1 | custom fusion | flops 720896 | bytes 8651456 | tf_op jit(solution)/shard_map/while/body/eval_jaxpr/scatter-add | solution.py:173
  515.9 18.4 %scatter_fusion.1 = f32[24,64,64]{2,1,0:T(8,128)S(1)} fusion(f32[24,64,64]{2,1,0:T(8,128)S(1)} %bitcast.297, s32[176]{0:T(256)S(1)} %reshape.627, f32[176,64,64]{2,1,0:T(8,128)} %bitcast.303), kind=kCustom, calls=%fused_computation.6.clone.1 | custom fusion | flops 720896 | bytes 8651456 | tf_op jit(solution)/shard_map/while/body/eval_jaxpr/scatter-add | solution.py:170
  539.6 18.4 %scatter_fusion = f32[24,64,64]{2,1,0:T(8,128)S(1)} fusion(f32[24,64,64]{2,1,0:T(8,128)S(1)} %bitcast.296, s32[176]{0:T(256)S(1)} %reshape.627, f32[176,64,64]{2,1,0:T(8,128)} %bitcast.302), kind=kCustom, calls=%fused_computation.7.clone.1 | custom fusion | flops 720896 | bytes 8651456 | tf_op jit(solution)/shard_map/while/body/eval_jaxpr/scatter-add | solution.py:173
  591.0 8.3 fusion.198
  599.3 18.4 %scatter_fusion.1 = f32[24,64,64]{2,1,0:T(8,128)S(1)} fusion(f32[24,64,64]{2,1,0:T(8,128)S(1)} %bitcast.297, s32[176]{0:T(256)S(1)} %reshape.627, f32[176,64,64]{2,1,0:T(8,128)} %bitcast.303), kind=kCustom, calls=%fused_computation.6.clone.1 | custom fusion | flops 720896 | bytes 8651456 | tf_op jit(solution)/shard_map/while/body/eval_jaxpr/scatter-add | solution.py:170
  623.1 18.4 %scatter_fusion = f32[24,64,64]{2,1,0:T(8,128)S(1)} fusion(f32[24,64,64]{2,1,0:T(8,128)S(1)} %bitcast.296, s32[176]{0:T(256)S(1)} %reshape.627, f32[176,64,64]{2,1,0:T(8,128)} %bitcast.302), kind=kCustom, calls=%fused_computation.7.clone.1 | custom fusion | flops 720896 | bytes 8651456 | tf_op jit(solution)/shard_map/while/body/eval_jaxpr/scatter-add | solution.py:173
  647.6 39.1 %all_to_all.62 = bf16[1536,3,256]{2,1,0:T(4,128)(2,1)S(1)} all-to-all(bf16[1536,3,256]{2,1,0:T(4,128)(2,1)S(1)} %copy.189), channel_id=1, replica_groups=mesh['seq'=4,'fsdp'=8] {'seq'}, dimensions={0} | all-to-all | bytes 4718592 | tf_op jit(solution)/shard_map/all_to_all | solution.py:306
  699.5 12.4 fusion.78
  713.4 10.2 fusion.95
  723.7 101.2 %reduce-scatter.5.cloned.1.call-done = f32[128,3072]{1,0:T(8,128)} async-done(((f32[1024,3072]{1,0:T(8,128)}), f32[128,3072]{1,0:T(8,128)}) %reduce-scatter.5.cloned.1.call-update) | async-done | bytes 1572880 | tf_op jit(solution)/shard_map/reduce_scatter | solution.py:316
  824.9 169.0 %reduce-scatter.11.cloned.1.call-done = f32[512,1024]{1,0:T(8,128)} async-done(((f32[4096,1024]{1,0:T(8,128)}), f32[512,1024]{1,0:T(8,128)}) %reduce-scatter.11.cloned.1.call-update) | async-done | bytes 2097168 | tf_op jit(solution)/shard_map/reduce_scatter | solution.py:275
  993.9 169.0 %reduce-scatter.9.cloned.1.call-done = f32[128,4096]{1,0:T(8,128)} async-done(((f32[1024,4096]{1,0:T(8,128)}), f32[128,4096]{1,0:T(8,128)}) %reduce-scatter.9.cloned.1.call-update) | async-done | bytes 2097168 | tf_op jit(solution)/shard_map/reduce_scatter | solution.py:273
  1165.4 9.3 all-gather.6
  1174.7 10.5 fusion.71
  1193.7 26.7 %all-reduce.6 = (f32[1024]{0:T(1024)S(1)}, f32[1024]{0:T(1024)S(1)}, f32[1024]{0:T(1024)S(1)}, f32[1024]{0:T(1024)S(1)}, f32[4096]{0:T(1024)S(1)}, /*index=5*/f32[1024]{0:T(1024)S(1)}) all-reduce(f32[1024]{0:T(1024)S(1)} %get-tuple-element.315, f32[1024]{0:T(1024)S(1)} %get-tuple-element.318, ...), channel_id=3, replica_groups=mesh['seq'=4,'fsdp'=8] {'fsdp'}, use_global_device_ids=true, to_apply=%region_21.22.clone | all-reduce | flops 9216 | bytes 73728
  1220.8 11.4 all-reduce.7
  1232.3 72.6 %all-reduce.11.cloned.1.call-done = (f32[128,3072]{1,0:T(8,128)}, f32[128,1024]{1,0:T(8,128)}, f32[128,4096]{1,0:T(8,128)}, f32[512,1024]{1,0:T(8,128)}) async-done(((f32[128,3072]{1,0:T(8,128)}, f32[128,1024]{1,0:T(8,128)}, f32[128,4096]{1,0:T(8,128)}, f32[512,1024]{1,0:T(8,128)}), (f32[128,3072]{1,0:T(8,128)}, f32[128,1024]{1,0:T(8,128)}, f32[128,4096]{1,0:T(8,128)}, ...) | async-done | bytes 6291472 | tf_op jit(solution)/shard_map/psum | solution.py:320
  (574 shorter events, 347.1 us)
Async XLA Ops:
  7.2 26.0 %copy-start.2 = (bf16[1,384,1024]{2,1,0:T(8,128)(2,1)S(1)}, bf16[1,384,1024]{2,1,0:T(8,128)(2,1)}, u32[]{:S(2)}) copy-start(bf16[1,384,1024]{2,1,0:T(8,128)(2,1)} %param.18) | copy-start | bytes 2359300
  7.2 70.0 %all-gather.12.cloned.1.call-start = ((), (), s32[]{:S(2)}) async-start(), calls=%async_computation.8 | async-start | bytes 7077888 | tf_op jit(solution)/shard_map/all_gather | solution.py:202
  7.9 245.5 %all-gather.14.cloned.1.call-start = ((), (), s32[]{:S(2)}) async-start(), calls=%async_computation.9 | async-start | bytes 2359296 | tf_op jit(solution)/shard_map/all_gather | solution.py:203
  8.7 247.8 %all-gather.16.cloned.1.call-start = ((), (), s32[]{:S(2)}) async-start(), calls=%async_computation.10 | async-start | bytes 9437184 | tf_op jit(solution)/shard_map/all_gather | solution.py:208
  23.0 54.2 %copy-start.31 = (f32[8,1,128]{2,1,0:T(1,128)}, f32[8,1,128]{2,1,0:T(1,128)S(1)}, u32[]{:S(2)}) copy-start(f32[8,1,128]{2,1,0:T(1,128)S(1)} %convert_element_type.130) | copy-start | bytes 12292
  31.8 45.4 %copy-start.33 = (f32[8,1,128]{2,1,0:T(1,128)}, f32[8,1,128]{2,1,0:T(1,128)S(1)}, u32[]{:S(2)}) copy-start(f32[8,1,128]{2,1,0:T(1,128)S(1)} %convert_element_type.131) | copy-start | bytes 12292
  33.1 44.1 %copy-start.37 = (f32[384]{0:T(512)}, f32[384]{0:T(512)S(1)}, u32[]{:S(2)}) copy-start(f32[384]{0:T(512)S(1)} %broadcast_multiply_fusion.1) | copy-start | bytes 4612
  34.1 43.1 %copy-start.41 = (f32[384]{0:T(512)}, f32[384]{0:T(512)S(1)}, u32[]{:S(2)}) copy-start(f32[384]{0:T(512)S(1)} %fusion.92) | copy-start | bytes 4612
  90.8 43.7 %copy-start.50 = (s32[4,22,3]{1,0,2:T(4,128)S(1)}, s32[4,22,3]{1,0,2:T(4,128)}, u32[]{:S(2)}) copy-start(s32[4,22,3]{1,0,2:T(4,128)} %param.20) | copy-start | bytes 3172
  90.8 43.8 %copy-start.55 = (s32[22,2]{0,1:T(2,128)S(1)}, s32[22,2]{0,1:T(2,128)}, u32[]{:S(2)}) copy-start(s32[22,2]{0,1:T(2,128)} %constant.106.clone.1) | copy-start | bytes 532
  90.8 44.1 %all-to-all-start = ((bf16[384,3,1024]{0,1,2:T(4,128)(2,1)}), bf16[384,3,1024]{0,1,2:T(4,128)(2,1)S(1)}, u32[]{:S(2)}, u32[]{:S(2)}) async-start(bf16[384,3,1024]{0,1,2:T(4,128)(2,1)} %copy.169), calls=%async_computation | async-start | bytes 6291456 | tf_op jit(solution)/shard_map/all_to_all | solution.py:224
  94.6 177.4 %all-gather.18.cloned.1.call-start = ((), (), s32[]{:S(2)}) async-start(), calls=%async_computation.11 | async-start | bytes 9437184 | tf_op jit(solution)/shard_map/all_gather | solution.py:210
  216.0 14.1 %copy-start.57 = (bf16[128]{0:T(256)(128)(2,1)S(1)}, bf16[128]{0:T(256)(128)(2,1)}, u32[]{:S(2)}) copy-start(bf16[128]{0:T(256)(128)(2,1)} %param.26) | copy-start | bytes 772
  216.0 37.4 %copy-start.3 = (bf16[1,384,1024]{2,1,0:T(8,128)(2,1)S(1)}, bf16[1,384,1024]{2,1,0:T(8,128)(2,1)}, u32[]{:S(2)}) copy-start(bf16[1,384,1024]{2,1,0:T(8,128)(2,1)} %param.18) | copy-start | bytes 2359300
  217.2 36.2 %all-to-all-start.1 = ((bf16[4,384,256]{1,2,0:T(8,128)(2,1)}), bf16[4,384,256]{1,2,0:T(8,128)(2,1)S(1)}, u32[]{:S(2)}, u32[]{:S(2)}) async-start(bf16[4,384,256]{1,2,0:T(8,128)(2,1)} %copy.179), calls=%async_computation.1 | async-start | bytes 1572864 | tf_op jit(solution)/shard_map/all_to_all | solution.py:238
  230.1 58.1 %copy-start.22 = (f32[8,1,128]{2,1,0:T(1,128)}, f32[8,1,128]{2,1,0:T(1,128)S(1)}, u32[]{:S(2)}) copy-start(f32[8,1,128]{2,1,0:T(1,128)S(1)} %convert_element_type.132) | copy-start | bytes 12292
  240.4 16.1 %copy-start.26 = (f32[8,1,128]{2,1,0:T(1,128)}, f32[8,1,128]{2,1,0:T(1,128)S(1)}, u32[]{:S(2)}) copy-start(f32[8,1,128]{2,1,0:T(1,128)S(1)} %convert_element_type.133) | copy-start | bytes 12292
  256.1 32.1 %copy-start.5 = (f32[384,1024]{1,0:T(8,128)}, f32[384,1024]{1,0:T(8,128)S(1)}, u32[]{:S(2)}) copy-start(f32[384,1024]{1,0:T(8,128)S(1)} %get-tuple-element.416) | copy-start | bytes 4718596
  256.1 32.1 %copy-start.35 = (f32[384]{0:T(512)}, f32[384]{0:T(512)S(1)}, u32[]{:S(2)}) copy-start(f32[384]{0:T(512)S(1)} %broadcast_multiply_fusion) | copy-start | bytes 4612
  256.4 31.8 %copy-start.39 = (f32[384]{0:T(512)}, f32[384]{0:T(512)S(1)}, u32[]{:S(2)}) copy-start(f32[384]{0:T(512)S(1)} %fusion.93) | copy-start | bytes 4612
  256.5 15.5 %copy-start.12 = (bf16[1,384,1024]{2,1,0:T(8,128)(2,1)S(1)}, bf16[1,384,1024]{2,1,0:T(8,128)(2,1)}, u32[]{:S(2)}) copy-start(bf16[1,384,1024]{2,1,0:T(8,128)(2,1)} %param.31) | copy-start | bytes 2359300
  272.0 11.9 copy-start.59
  292.6 15.0 %all-to-all-start.2 = ((bf16[384,4,256]{0,2,1:T(8,128)(2,1)}), bf16[384,4,256]{0,2,1:T(8,128)(2,1)S(1)}, u32[]{:S(2)}, u32[]{:S(2)}) async-start(bf16[384,4,256]{0,2,1:T(8,128)(2,1)} %bitcast.63), calls=%async_computation.2 | async-start | bytes 1572864 | tf_op jit(solution)/shard_map/all_to_all | solution.py:285
  296.3 427.4 %reduce-scatter.7.cloned.1.call-start = ((), (), s32[]{:S(2)}) async-start(), calls=%async_computation.13 | async-start | bytes 4718592 | tf_op jit(solution)/shard_map/reduce_scatter | solution.py:317
  299.6 525.3 %reduce-scatter.5.cloned.1.call-start = ((), (), s32[]{:S(2)}) async-start(), calls=%async_computation.12 | async-start | bytes 14155776 | tf_op jit(solution)/shard_map/reduce_scatter | solution.py:316
  309.4 10.7 copy-start.48
  392.9 10.7 copy-start.48
  476.4 10.7 copy-start.48
  559.9 10.7 copy-start.48
  698.4 295.5 %reduce-scatter.11.cloned.1.call-start = ((), (), s32[]{:S(2)}) async-start(), calls=%async_computation.15 | async-start | bytes 18874368 | tf_op jit(solution)/shard_map/reduce_scatter | solution.py:275
  712.0 450.9 %reduce-scatter.9.cloned.1.call-start = ((), (), s32[]{:S(2)}) async-start(), calls=%async_computation.14 | async-start | bytes 18874368 | tf_op jit(solution)/shard_map/reduce_scatter | solution.py:273
  723.6 581.3 %all-reduce.11.cloned.1.call-start = ((), (), s32[]{:S(2)}) async-start(), calls=%async_computation.16 | async-start | bytes 12582912 | tf_op jit(solution)/shard_map/psum | solution.py:320
  (77 other events, 289.4 us)
Sparse Core Ops, SparseCore 0:
  9.7 67.4 all-gather.11
  78.8 27.6 all-gather.13
  108.1 81.6 all-gather.15
  191.3 80.6 all-gather.17
  299.7 49.0 reduce-scatter.6
  698.6 126.3 reduce-scatter.4
  827.3 166.5 reduce-scatter.10
  996.2 166.5 reduce-scatter.8
  1166.6 138.2 all-reduce.10
where the time goes:
time: 1330 us; the launch traced here: 1320 us
  waiting for transfers between devices  572 us (43%)
  matrix products  213 us (16%)
  blocking collectives  181 us (14%)
  other arithmetic  168 us (13%)
  local copies, waits for them, and re-layouts  156 us (12%)
  between operations  16 us (1%)
    reduce_scatter x1, waiting for transfers between devices, per_device(): lax.psum_scatter(grad_in, 'fsdp', scatter_dimension=0, tiled=True)  169 us
    reduce_scatter x1, waiting for transfers between devices, per_device(): lax.psum_scatter(grad_down, 'fsdp', scatter_dimension=0, tiled=True)  169 us
    reduce_scatter x1, waiting for transfers between devices, per_device(): lax.psum_scatter(grad_qkv, 'fsdp', scatter_dimension=0, tiled=True)  101 us
    scatter-add x4, other arithmetic, head_backward(): lead_dot(edge_low, grad_edge).reshape(blocks, BLK, DH).at[block_list]  73.5 us
    scatter-add x4, other arithmetic, head_backward(): grad_keys = lead_dot(grad_edge_scores, edge_queries).reshape(blocks, BLK,...  73.5 us
    psum x1, waiting for transfers between devices, per_device(): lax.psum((shares[0], shares[1], shares[2], shares[3], shares[4], shares[5...  72.6 us
    all_gather x1, waiting for transfers between devices, per_device(): lax.all_gather(w_qkv, 'fsdp', axis=0, tiled=True)  43.1 us
    all_to_all x1, blocking collectives, per_device(): lax.all_to_all(grad_heads, 'seq', split_axis=0, concat_axis=2, tiled=True)  39.1 us
  transfers between devices with their start and end apart: 12, of which 7 were waited for; matrix products, arithmetic and copies ran while one was open for 38% of the time, Pallas kernels for 0%

commit v1 on v0

v1 whole, which is shorter than its diff:
```python
import functools
import math

import jax
import jax.numpy as jnp
from jax import lax
from jax.experimental import pallas as pl
from jax.experimental.pallas import tpu as pltpu
from jax.sharding import PartitionSpec as P

DH = 64
BLK = 64
LANES = 128
NEG = -1e30
F32 = jnp.float32
BF16 = jnp.bfloat16


def layer_norm_parts(rows):
    center = rows - jnp.mean(rows, axis=-1, keepdims=True)
    variance = jnp.mean(center * center, axis=-1, keepdims=True)
    inv = lax.rsqrt(variance + 1e-05)
    return center * inv, inv


def gelu_tanh(pre_act):
    return (
        0.5
        * pre_act
        * (1.0 + jnp.tanh(0.7978845608028654 * (pre_act + 0.044715 * pre_act * pre_act * pre_act)))
    )


def dot_nn(a, b):
    return jnp.dot(a, b, preferred_element_type=F32)


def dot_nt(a, b):
    return lax.dot_general(a, b, (((1,), (1,)), ((), ())), preferred_element_type=F32)


def dot_tn(a, b):
    return lax.dot_general(a, b, (((0,), (0,)), ((), ())), preferred_element_type=F32)


def mask_features(random_blocks, seq_ids, docs):
    heads, inner, _ = random_blocks.shape
    blocks = inner + 2
    length = seq_ids.shape[0]
    ids = jnp.arange(blocks, dtype=jnp.int32)
    near = jnp.abs(ids[:, None] - ids[None, :]) <= 1
    edge = (ids == 0) | (ids == blocks - 1)
    fixed = near | edge[:, None] | edge[None, :]
    picked = jnp.any(random_blocks[:, :, :, None] == ids, axis=2)
    picked = jnp.pad(picked, ((0, 0), (1, 1), (0, 0)))
    used = fixed[None] | picked
    block_part = jnp.where(used, 0.0, NEG).astype(BF16)
    block_part = jnp.repeat(block_part, length // blocks, axis=1)
    doc_ids = jnp.arange(docs, dtype=jnp.int32)
    own_doc = seq_ids[:, None] == doc_ids[None, :]
    doc_part = jnp.where(own_doc, NEG, 0.0).astype(BF16)
    doc_part = jnp.broadcast_to(doc_part, (heads,) + doc_part.shape)
    spare = jnp.zeros((heads, length, DH - blocks - docs), BF16)
    query_half = jnp.concatenate([block_part, doc_part, spare], axis=-1)
    block_hot = (jnp.arange(length, dtype=jnp.int32)[:, None] // (length // blocks)) == ids[None, :]
    key_half = jnp.concatenate(
        [
            block_hot.astype(BF16),
            jnp.where(own_doc, 0.0, 1.0).astype(BF16),
            jnp.zeros((length, DH - blocks - docs), BF16),
        ],
        axis=-1,
    )
    return (
        jnp.concatenate([query_half, query_half], axis=-1),
        jnp.concatenate([key_half, key_half], axis=-1),
    )


def own_lanes(odd, shape):
    lane = lax.broadcasted_iota(jnp.int32, shape, 1)
    return (lane >= DH) if odd else (lane < DH)


def attend_forward(tile, q_ref, k_ref, v_ref, qf_ref, kf_ref, out_ref, lse_ref):
    length = k_ref.shape[0]
    scale = jnp.asarray(1.0 / math.sqrt(DH), BF16)
    values_t = v_ref[...].T
    for odd in (0, 1):
        mine = own_lanes(odd, (length, LANES))
        keys = jnp.where(mine, k_ref[...], kf_ref[...])
        for start in range(0, length, tile):
            rows = pl.ds(start, tile)
            lanes = own_lanes(odd, (tile, LANES))
            queries = jnp.where(lanes, q_ref[rows, :] * scale, qf_ref[odd, rows, :])
            scores = dot_nt(keys, queries)
            top = jnp.max(scores, axis=0, keepdims=True)
            prob = jnp.exp(scores - top)
            total = jnp.sum(prob, axis=0, keepdims=True)
            mixed = dot_nn(values_t, prob.astype(BF16)) / total
            lse_ref[0, odd, rows] = (top + jnp.log(total))[0]
            result = mixed.T.astype(BF16)
            if odd:
                out_ref[rows, :] = jnp.where(lanes, result, out_ref[rows, :])
            else:
                out_ref[rows, :] = result


def attend_backward(
    tile, q_ref, k_ref, v_ref, qf_ref, kf_ref, go_ref, lse_ref, dq_ref, dk_ref, dv_ref, p_sc, s_sc
):
    length = k_ref.shape[0]
    scale = jnp.asarray(1.0 / math.sqrt(DH), BF16)
    keys_t = k_ref[...].T
    for odd in (0, 1):
        mine = own_lanes(odd, (length, LANES))
        keys = jnp.where(mine, k_ref[...], kf_ref[...])
        values = jnp.where(mine, v_ref[...], jnp.zeros((), BF16))
        for start in range(0, length, tile):
            rows = pl.ds(start, tile)
            lanes = own_lanes(odd, (tile, LANES))
            queries = jnp.where(lanes, q_ref[rows, :] * scale, qf_ref[odd, rows, :])
            prob = jnp.exp(dot_nt(keys, queries) - lse_ref[0, odd, rows][None, :])
            grad_prob = dot_nt(values, go_ref[rows, :])
            delta = jnp.sum(prob * grad_prob, axis=0, keepdims=True)
            p_sc[:, rows] = prob.astype(BF16)
            s_sc[:, rows] = (prob * (grad_prob - delta)).astype(BF16)
        grad_v = dot_nn(p_sc[...], go_ref[...]).astype(BF16)
        grad_k = dot_nn(s_sc[...], q_ref[...] * scale).astype(BF16)
        grad_q = (dot_nn(keys_t, s_sc[...]) * (1.0 / math.sqrt(DH))).T.astype(BF16)
        if odd:
            dv_ref[...] = jnp.where(mine, grad_v, dv_ref[...])
            dk_ref[...] = jnp.where(mine, grad_k, dk_ref[...])
            dq_ref[...] = jnp.where(mine, grad_q, dq_ref[...])
        else:
            dv_ref[...] = grad_v
            dk_ref[...] = grad_k
            dq_ref[...] = grad_q


def column_spec(length, offset):
    return pl.BlockSpec((length, LANES), lambda p: (0, p + offset))


def attention_forward(by_heads, query_feats, key_feats):
    length = by_heads.shape[0]
    heads = query_feats.shape[0]
    pairs = heads // 2
    return pl.pallas_call(
        functools.partial(attend_forward, 256),
        grid=(pairs,),
        out_shape=(
            jax.ShapeDtypeStruct((length, heads * DH), BF16),
            jax.ShapeDtypeStruct((pairs, 2, length), F32),
        ),
        in_specs=[
            column_spec(length, 0),
            column_spec(length, pairs),
            column_spec(length, 2 * pairs),
            pl.BlockSpec((2, length, LANES), lambda p: (p, 0, 0)),
            pl.BlockSpec((length, LANES), lambda p: (0, 0)),
        ],
        out_specs=(
            column_spec(length, 0),
            pl.BlockSpec((1, 2, length), lambda p: (p, 0, 0)),
        ),
        compiler_params=pltpu.CompilerParams(vmem_limit_bytes=56 << 20),
        cost_estimate=pl.CostEstimate(
            flops=heads * length * length * 512, bytes_accessed=8 << 20, transcendentals=heads * length * length
        ),
    )(by_heads, by_heads, by_heads, query_feats, key_feats)


def attention_backward(by_heads, query_feats, key_feats, grad_out, lse):
    length = by_heads.shape[0]
    heads = query_feats.shape[0]
    pairs = heads // 2
    shape = jax.ShapeDtypeStruct((length, heads * DH), BF16)
    return pl.pallas_call(
        functools.partial(attend_backward, 256),
        grid=(pairs,),
        out_shape=(shape, shape, shape),
        in_specs=[
            column_spec(length, 0),
            column_spec(length, pairs),
            column_spec(length, 2 * pairs),
            pl.BlockSpec((2, length, LANES), lambda p: (p, 0, 0)),
            pl.BlockSpec((length, LANES), lambda p: (0, 0)),
            column_spec(length, 0),
            pl.BlockSpec((1, 2, length), lambda p: (p, 0, 0)),
        ],
        out_specs=(column_spec(length, 0), column_spec(length, 0), column_spec(length, 0)),
        scratch_shapes=[pltpu.VMEM((length, length), BF16), pltpu.VMEM((length, length), BF16)],
        compiler_params=pltpu.CompilerParams(vmem_limit_bytes=56 << 20),
        cost_estimate=pl.CostEstimate(
            flops=heads * length * length * 1280, bytes_accessed=12 << 20, transcendentals=heads * length * length
        ),
    )(by_heads, by_heads, by_heads, query_feats, key_feats, grad_out, lse)


def swap_thirds(rows, outer, inner):
    count, width = rows.shape
    return rows.reshape(count, outer, inner, width // (outer * inner)).swapaxes(1, 2).reshape(count, width)


def per_device(
    seq_count,
    fsdp_count,
    tokens,
    segment_ids,
    random_blocks,
    ln1_gain,
    ln1_bias,
    w_qkv,
    w_out,
    ln2_gain,
    ln2_bias,
    w_in,
    b_in,
    w_down,
    b_down,
    cotangent,
):
    gather = functools.partial(lax.all_gather, axis_name="fsdp", axis=0, tiled=True)
    width = w_qkv.shape[1] // 3
    share = ln1_gain.shape[0]
    packed = jnp.concatenate([ln1_gain, ln1_bias, ln2_gain, ln2_bias, b_down, b_in])[None]
    packed = gather(packed).astype(F32)
    gain_one, bias_one, gain_two, bias_two, down_bias = (
        packed[:, i * share : (i + 1) * share].reshape(-1) for i in range(5)
    )
    in_bias = packed[:, 5 * share :].reshape(-1)
    qkv_weight = gather(swap_thirds(w_qkv, 3, seq_count))
    seq_ids = lax.all_gather(segment_ids[0], "seq", axis=0, tiled=True)
    out_weight = gather(w_out)
    in_weight = gather(w_in)
    down_weight = gather(w_down)
    query_feats, key_feats = mask_features(random_blocks, seq_ids, 6)

    token_rows = tokens[0].astype(F32)
    hat_one, inv_one = layer_norm_parts(token_rows)
    normed_one = (hat_one * gain_one + bias_one).astype(BF16)
    qkv_rows = dot_nn(normed_one, qkv_weight).astype(BF16)
    by_heads = lax.all_to_all(qkv_rows, "seq", split_axis=1, concat_axis=0, tiled=True)
    att_heads, lse = attention_forward(by_heads, query_feats, key_feats)
    att_rows = lax.all_to_all(att_heads, "seq", split_axis=0, concat_axis=1, tiled=True)
    hidden = token_rows + dot_nn(att_rows, out_weight)
    hat_two, inv_two = layer_norm_parts(hidden)
    normed_two = (hat_two * gain_two + bias_two).astype(BF16)
    pre_act = dot_nn(normed_two, in_weight) + in_bias
    act_value, pull_gelu = jax.vjp(gelu_tanh, pre_act)
    act_low = act_value.astype(BF16)
    result = hidden + dot_nn(act_low, down_weight) + down_bias

    cot_low = cotangent[0]
    cot_rows = cot_low.astype(F32)
    grad_pre = pull_gelu(dot_nt(cot_low, down_weight))[0].astype(BF16)
    grad_norm_two = dot_nt(grad_pre, in_weight)
    scaled = grad_norm_two * gain_two
    grad_hidden = cot_rows + inv_two * (
        scaled
        - jnp.mean(scaled, axis=-1, keepdims=True)
        - hat_two * jnp.mean(scaled * hat_two, axis=-1, keepdims=True)
    )
    hidden_low = grad_hidden.astype(BF16)
    grad_att = dot_nt(hidden_low, out_weight).astype(BF16)
    grad_att_heads = lax.all_to_all(grad_att, "seq", split_axis=1, concat_axis=0, tiled=True)
    scatter = functools.partial(
        lax.psum_scatter, axis_name="fsdp", scatter_dimension=0, tiled=True
    )
    share_down = scatter(dot_tn(act_low, cot_low).astype(BF16))
    share_in = scatter(dot_tn(normed_two, grad_pre).astype(BF16))
    share_out = scatter(dot_tn(att_rows, hidden_low).astype(BF16))
    grad_heads = jnp.concatenate(
        attention_backward(by_heads, query_feats, key_feats, grad_att_heads, lse), axis=1
    )
    grad_qkv_rows = lax.all_to_all(grad_heads, "seq", split_axis=0, concat_axis=1, tiled=True)
    share_qkv = scatter(dot_tn(normed_one, grad_qkv_rows).astype(BF16))
    grad_norm_one = dot_nt(grad_qkv_rows, qkv_weight)
    scaled_one = grad_norm_one * gain_one
    grad_tokens = (
        grad_hidden
        + inv_one
        * (
            scaled_one
            - jnp.mean(scaled_one, axis=-1, keepdims=True)
            - hat_one * jnp.mean(scaled_one * hat_one, axis=-1, keepdims=True)
        )
    ).astype(BF16)

    small = [
        jnp.sum(grad_norm_one * hat_one, axis=0),
        jnp.sum(grad_norm_one, axis=0),
        jnp.sum(grad_norm_two * hat_two, axis=0),
        jnp.sum(grad_norm_two, axis=0),
        jnp.sum(cot_rows, axis=0),
        jnp.sum(grad_pre.astype(F32), axis=0),
    ]
    small = jnp.concatenate([v.reshape(fsdp_count, -1) for v in small], axis=1)
    small = lax.psum(small, ("seq", "fsdp"))
    small = lax.dynamic_index_in_dim(small, lax.axis_index("fsdp"), 0, keepdims=False)
    parts = [small[i * share : (i + 1) * share] for i in range(5)] + [small[5 * share :]]
    total_down, total_in, total_out, total_qkv = lax.psum(
        (share_down, share_in, share_out, share_qkv), "seq"
    )
    return (
        result.astype(BF16)[None],
        grad_tokens[None],
        parts[0],
        parts[1],
        swap_thirds(total_qkv, seq_count, 3).astype(F32),
        total_out.astype(F32),
        parts[2],
        parts[3],
        total_in.astype(F32),
        parts[5],
        total_down.astype(F32),
        parts[4],
    )


def solution(mesh):
    return jax.shard_map(
        functools.partial(per_device, mesh.shape["seq"], mesh.shape["fsdp"]),
        mesh=mesh,
        in_specs=(
            P("fsdp", "seq", None),
            P("fsdp", "seq"),
            P("seq", None, None),
            P("fsdp"),
            P("fsdp"),
            P("fsdp", None),
            P("fsdp", None),
            P("fsdp"),
            P("fsdp"),
            P("fsdp", None),
            P("fsdp"),
            P("fsdp", None),
            P("fsdp"),
            P("fsdp", "seq", None),
        ),
        out_specs=(
            P("fsdp", "seq", None),
            P("fsdp", "seq", None),
            P("fsdp"),
            P("fsdp"),
            P("fsdp", None),
            P("fsdp", None),
            P("fsdp"),
            P("fsdp"),
            P("fsdp", None),
            P("fsdp"),
            P("fsdp", None),
            P("fsdp"),
        ),
        check_vma=False,
    )
```

time: 1330 us -> 775 us (0.58)
  other arithmetic: 168 us -> 12.4 us
  waiting for transfers between devices: 572 us -> 427 us
  matrix products: 213 us -> 83.1 us
  local copies, waits for them, and re-layouts: 156 us -> 38 us
  Pallas kernels: 0 us -> 52.6 us
  blocking collectives: 181 us -> 132 us
    reduce_scatter x4, waiting for transfers between devices: 439 us -> 256 us  [the longest x1 90.5 us: per_device(): share_in = scatter(dot_tn(normed_two, grad_pre).astype(BF16))]
    scatter-add x8 -> x0, other arithmetic: 147 us -> none  [the longest x4 73.5 us: head_backward(): lead_dot(edge_low, grad_edge).reshape(blocks, BLK, DH).at[block_list]]
    all_gather x4, waiting for transfers between devices: 49.3 us -> 130 us  [the longest x1 73.1 us: per_device(): down_weight = gather(w_down)]
    dot_general x52 -> x12, matrix products: 156 us -> 83.1 us  [the longest x4 29.8 us: dot_tn(): lax.dot_general(a, b, (((0,), (0,)), ((), ())), preferred_element_type=F32)]
    reshape x16 -> x0, matrix products: 56.6 us -> none  [the longest x4 33.1 us: head_backward(): grad_near_keys = jnp.einsum('onm,ons->oms', score_gradient, blocked_queri...]
    pallas_call x0 -> x2, Pallas kernels: none -> 52.6 us  [the longest x1 27.9 us: attention_backward(): pl.pallas_call(functools.partial(attend_backward, 256), grid=(pairs,), ou...]
    all_gather x6 -> x1, blocking collectives: 64.3 us -> 15.7 us  [per_device(): packed = gather(packed).astype(F32)]
    psum x1, waiting for transfers between devices: 72.6 us -> 30 us  [per_device(): lax.psum((share_down, share_in, share_out, share_qkv), 'seq')]
  transfers between devices with their start and end apart: 12 -> 11, of which waited for: 7 -> 9; matrix products, arithmetic and copies ran while one was open for 38% -> 12% of each run, Pallas kernels for 0% -> 3%
where the time goes in v1:
time: 775 us; the launch traced here: 769 us
  waiting for transfers between devices  427 us (55%)
  blocking collectives  132 us (17%)
  matrix products  83.1 us (11%)
  Pallas kernels  52.6 us (7%)
  local copies, waits for them, and re-layouts  38 us (5%)
  between operations  14.7 us (2%)
  other arithmetic  12.4 us (2%)
  starting transfers between devices  9.14 us (1%)
    reduce_scatter x1, waiting for transfers between devices, per_device(): share_in = scatter(dot_tn(normed_two, grad_pre).astype(BF16))  90.5 us
    reduce_scatter x1, waiting for transfers between devices, per_device(): share_down = scatter(dot_tn(act_low, cot_low).astype(BF16))  90.3 us
    all_gather x1, waiting for transfers between devices, per_device(): down_weight = gather(w_down)  73.1 us
    all_gather x1, waiting for transfers between devices, per_device(): qkv_weight = gather(swap_thirds(w_qkv, 3, seq_count))  48 us
    reduce_scatter x1, waiting for transfers between devices, per_device(): share_qkv = scatter(dot_tn(normed_one, grad_qkv_rows).astype(BF16))  42.7 us
    psum x1, blocking collectives, per_device(): small = lax.psum(small, ('seq', 'fsdp'))  38.9 us
    reduce_scatter x1, waiting for transfers between devices, per_device(): share_out = scatter(dot_tn(att_rows, hidden_low).astype(BF16))  32.6 us
    all_to_all x1, blocking collectives, per_device(): lax.all_to_all(grad_heads, 'seq', split_axis=0, concat_axis=1, tiled=True)  31.1 us
  transfers between devices with their start and end apart: 11, of which 9 were waited for; matrix products, arithmetic and copies ran while one was open for 12% of the time, Pallas kernels for 3%

profile of v1, /device:TPU:0, one launch (start us, length us, event | category | flops | bytes accessed | tf_op | source)
XLA Modules:
  0.0 769.1 jit_solution(5318237319889478698)
XLA Ops:
  13.2 15.7 %all-gather.2 = bf16[8,1,1152]{2,1,0:T(2,128)(2,1)S(1)} all-gather(bf16[1,1,1152]{2,1,0:T(2,128)(2,1)S(1)} %reshape.256), channel_id=2, replica_groups=mesh['seq'=4,'fsdp'=8] {'fsdp'}, dimensions={0}, use_global_device_ids=true | all-gather | bytes 20736 | tf_op jit(solution)/shard_map/all_gather | solution.py:228
  30.2 48.0 %all-gather.8.cloned.1.call-done = bf16[1024,3072]{0,1:T(8,128)(2,1)} async-done(((bf16[128,3072]{0,1:T(8,128)(2,1)}), bf16[1024,3072]{0,1:T(8,128)(2,1)}) %all-gather.8.cloned.1.call-update) | async-done | bytes 6291472 | tf_op jit(solution)/shard_map/all_gather | solution.py:233
  78.2 7.4 convolution_convert_fusion.3
  87.2 4.6 all-to-all-start
  92.2 31.0 %all-gather.1 = s32[1,1536]{1,0:T(1,128)S(1)} all-gather(s32[1,384]{1,0:T(1,128)S(1)} %copy-done.18), channel_id=3, replica_groups=mesh['seq'=4,'fsdp'=8] {'seq'}, dimensions={1}, use_global_device_ids=true | all-gather | bytes 7680 | tf_op jit(solution)/shard_map/all_gather | solution.py:234
  125.3 9.9 %concatenate.20.qf_ref = bf16[4,1536,128]{2,1,0:T(8,128)(2,1)} concatenate(bf16[4,1536,24]{2,1,0:T(8,128)(2,1)S(1)} %bitcast.139, bf16[4,1536,6]{2,1,0:T(8,128)(2,1)S(1)} %broadcast_in_dim.66, bf16[4,1536,34]{2,1,0:T(8,128)(2,1)} %broadcast_in_dim.67, bf16[4,1536,24]{2,1,0:T(8,128)(2,1)S(1)} %bitcast.140, bf16[4,1536,6]{2,1,0:T(8,128)(2,1)S(1)} %broadcast_in_dim.66, ...), dimensions={2} | concatenate | bytes 3145728 | tf_op jit(solution)/shard_map/concatenate | solution.py:75
  137.6 24.7 %shard_map.229 = (bf16[1536,256]{1,0:T(8,128)(2,1)}, f32[2,2,1536]{2,1,0:T(2,128)}) custom-call(bf16[1536,768]{1,0:T(8,128)(2,1)} %bitcast.7.q_ref.k_ref.v_ref, bf16[1536,768]{1,0:T(8,128)(2,1)} %bitcast.7.q_ref.k_ref.v_ref, bf16[1536,768]{1,0:T(8,128)(2,1)} %bitcast.7.q_ref.k_ref.v_ref, bf16[4,1536,128]{2,1,0:T(8,128)(2,1)} %concatenate.20.qf_ref, ...), custom_call_target="tpu_custom_call" | custom-call | flops 4831838208 | bytes 8388608 | tf_op jit(solution)/shard_map/pallas_call | solution.py:149
  164.7 3.5 all-to-all-start.1
  169.4 9.0 %all-to-all-done.1 = bf16[4,384,256]{1,2,0:T(8,128)(2,1)S(1)} async-done(((bf16[4,384,256]{1,2,0:T(8,128)(2,1)}), bf16[4,384,256]{1,2,0:T(8,128)(2,1)S(1)}, u32[]{:S(2)}, u32[]{:S(2)}) %all-to-all-start.1) | async-done | bytes 786464 | tf_op jit(solution)/shard_map/all_to_all | solution.py:246
  178.3 3.0 fusion.54
  181.6 8.7 %all-gather.12.cloned.1.call-done = bf16[1024,4096]{1,0:T(8,128)(2,1)} async-done(((bf16[128,4096]{1,0:T(8,128)(2,1)}), bf16[1024,4096]{1,0:T(8,128)(2,1)}) %all-gather.12.cloned.1.call-update) | async-done | bytes 8388624 | tf_op jit(solution)/shard_map/all_gather | solution.py:236
  190.4 9.0 %convolution_add_fusion = f32[384,4096]{1,0:T(8,128)} fusion(bf16[1024,4096]{1,0:T(8,128)(2,1)} %all-gather.12.cloned.1.call-done, f32[4096]{0:T(1024)S(1)} %bitcast.157, f32[384,1024]{1,0:T(8,128)S(1)} %get-tuple-element.85, f32[1024]{0:T(1024)S(1)} %copy-done.15, f32[1024]{0:T(1024)S(1)} %get-tuple-element.77, f32[384]{0:T(512)S(1)} %add_rsqrt_fusion, ...), kind=kOutput, calls=%fused_computation.15 | convolution fusion | flops 3224764416 | bytes 16280576 | tf_op jit(solution)/shard_map/dot_general | solution.py:35
  199.4 73.1 %all-gather.14.cloned.1.call-done = bf16[4096,1024]{1,0:T(8,128)(2,1)} async-done(((bf16[512,1024]{1,0:T(8,128)(2,1)}), bf16[4096,1024]{1,0:T(8,128)(2,1)}) %all-gather.14.cloned.1.call-update) | async-done | bytes 8388624 | tf_op jit(solution)/shard_map/all_gather | solution.py:237
  272.5 11.3 %convert_reduce_fusion = (f32[4096]{0:T(1024)S(1)}, bf16[384,4096]{1,0:T(8,128)(2,1)S(1)}) fusion(f32[384,4096]{1,0:T(8,128)} %convolution_add_fusion, bf16[4096,1024]{1,0:T(8,128)(2,1)} %all-gather.14.cloned.1.call-done, bf16[1,384,1024]{2,1,0:T(8,128)(2,1)S(1)} %copy-done.9), kind=kOutput, calls=%fused_computation.12 | convolution fusion | flops 3262115840 | bytes 18628608 | tf_op jit(solution)/shard_map/dot_general | solution.py:39
  283.8 3.9 multiply_reduce_fusion
  290.4 15.5 %all_to_all.76 = bf16[384,4,256]{2,0,1:T(8,128)(2,1)} all-to-all(bf16[384,4,256]{2,0,1:T(8,128)(2,1)S(1)} %bitcast.145), channel_id=1, replica_groups=mesh['seq'=4,'fsdp'=8] {'seq'}, dimensions={1} | all-to-all | bytes 1572864 | tf_op jit(solution)/shard_map/all_to_all | solution.py:267
  305.9 27.9 %shard_map.230 = (bf16[1536,256]{1,0:T(8,128)(2,1)}, bf16[1536,256]{1,0:T(8,128)(2,1)}, bf16[1536,256]{1,0:T(8,128)(2,1)}) custom-call(bf16[1536,768]{1,0:T(8,128)(2,1)} %bitcast.7.q_ref.k_ref.v_ref, bf16[1536,768]{1,0:T(8,128)(2,1)} %bitcast.7.q_ref.k_ref.v_ref, bf16[1536,768]{1,0:T(8,128)(2,1)} %bitcast.7.q_ref.k_ref.v_ref, ...), custom_call_target="tpu_custom_call" | custom-call | flops 12079595520 | bytes 12582912 | tf_op jit(solution)/shard_map/pallas_call | solution.py:179
  333.9 3.2 pad_maximum_fusion
  337.1 4.3 copy.63
  341.4 31.1 %all_to_all.77 = bf16[4,384,768]{1,2,0:T(8,128)(2,1)S(1)} all-to-all(bf16[4,384,768]{1,2,0:T(8,128)(2,1)} %copy.63), channel_id=1, replica_groups=mesh['seq'=4,'fsdp'=8] {'seq'}, dimensions={0} | all-to-all | bytes 4718592 | tf_op jit(solution)/shard_map/all_to_all | solution.py:277
  373.9 5.9 convolution_convert_fusion.2
  379.8 3.7 convolution_convert_fusion.4
  383.6 8.9 %convolution_convert_fusion.1 = bf16[1024,4096]{1,0:T(8,128)(2,1)} fusion(bf16[384,4096]{1,0:T(8,128)(2,1)} %copy-done.26, f32[384,1024]{1,0:T(8,128)S(1)} %get-tuple-element.85, f32[1024]{0:T(1024)S(1)} %copy-done.15, f32[1024]{0:T(1024)S(1)} %get-tuple-element.77, f32[384]{0:T(512)S(1)} %add_rsqrt_fusion, f32[384]{0:T(512)S(1)} %broadcast_multiply_fusion.4), kind=kOutput, calls=%fused_computation.5 | convolution fusion | flops 3227385856 | bytes 13118464 | tf_op jit(solution)/shard_map/dot_general | solution.py:43
  392.6 11.3 %convolution_convert_fusion = bf16[4096,1024]{1,0:T(8,128)(2,1)} fusion(bf16[1,384,1024]{2,1,0:T(8,128)(2,1)} %param.27, f32[384,4096]{1,0:T(8,128)} %convolution_add_fusion), kind=kOutput, calls=%fused_computation.4 | convolution fusion | flops 3239575552 | bytes 15466496 | tf_op jit(solution)/shard_map/dot_general | solution.py:43
  404.2 42.7 %reduce-scatter.5.cloned.1.call-done = bf16[128,3072]{1,0:T(8,128)(2,1)} async-done(((bf16[1024,3072]{1,0:T(8,128)(2,1)}), bf16[128,3072]{1,0:T(8,128)(2,1)}) %reduce-scatter.5.cloned.1.call-update) | async-done | bytes 786448 | tf_op jit(solution)/shard_map/reduce_scatter | solution.py:278
  451.2 32.6 %reduce-scatter.7.cloned.1.call-done = bf16[128,1024]{1,0:T(8,128)(2,1)} async-done(((bf16[1024,1024]{1,0:T(8,128)(2,1)}), bf16[128,1024]{1,0:T(8,128)(2,1)}) %reduce-scatter.7.cloned.1.call-update) | async-done | bytes 262160 | tf_op jit(solution)/shard_map/reduce_scatter | solution.py:273
  483.8 90.5 %reduce-scatter.9.cloned.1.call-done = bf16[128,4096]{1,0:T(8,128)(2,1)} async-done(((bf16[1024,4096]{1,0:T(8,128)(2,1)}), bf16[128,4096]{1,0:T(8,128)(2,1)}) %reduce-scatter.9.cloned.1.call-update) | async-done | bytes 1048592 | tf_op jit(solution)/shard_map/reduce_scatter | solution.py:272
  574.3 90.3 %reduce-scatter.11.cloned.1.call-done = bf16[512,1024]{1,0:T(8,128)(2,1)} async-done(((bf16[4096,1024]{1,0:T(8,128)(2,1)}), bf16[512,1024]{1,0:T(8,128)(2,1)}) %reduce-scatter.11.cloned.1.call-update) | async-done | bytes 1048592 | tf_op jit(solution)/shard_map/reduce_scatter | solution.py:271
  664.7 10.0 %fusion.27 = bf16[1,384,1024]{2,1,0:T(8,128)(2,1)} fusion(f32[384,1024]{1,0:T(8,128)S(1)} %get-tuple-element.85, bf16[4096,1024]{1,0:T(8,128)(2,1)} %all-gather.14.cloned.1.call-done, f32[1024]{0:T(1024)S(1)} %copy-done.14, f32[384,4096]{1,0:T(8,128)} %convolution_add_fusion), kind=kOutput, calls=%fused_computation.55 | convolution fusion | flops 3236560896 | bytes 17043456 | tf_op jit(solution)/shard_map/dot_general | solution.py:35
  674.7 7.7 %fusion.21 = (f32[1024]{0:T(1024)S(1)}, f32[384]{0:T(512)S(1)}, f32[384]{0:T(512)S(1)}, f32[1024]{0:T(1024)S(1)}, f32[384,1024]{1,0:T(8,128)}) fusion(bf16[1,384,1024]{2,1,0:T(8,128)(2,1)} %param.14, f32[384]{0:T(512)S(1)} %add_rsqrt_fusion.1, f32[384]{0:T(512)S(1)} %broadcast_multiply_fusion.5, f32[1024]{0:T(1024)S(1)} %get-tuple-element.81, ...), kind=kOutput, calls=%fused_computation.40 | convolution fusion | flops 2419848192 | bytes 11028480 | tf_op jit(solution)/shard_map/dot_general | solution.py:39
  682.5 38.9 %psum.35 = f32[8,1152]{1,0:T(8,128)S(1)} all-reduce(f32[8,1152]{1,0:T(8,128)S(1)} %constant_dynamic-update-slice_fusion), channel_id=1, replica_groups=mesh['seq'=4,'fsdp'=8] {'seq','fsdp'}, use_global_device_ids=true, to_apply=%region_15.16 | all-reduce | flops 9216 | bytes 73728 | tf_op jit(solution)/shard_map/psum | solution.py:300
  725.5 30.0 %all-reduce.4.cloned.1.call-done = (bf16[128,3072]{0,1:T(8,128)(2,1)}, bf16[128,1024]{1,0:T(8,128)(2,1)}, bf16[128,4096]{1,0:T(8,128)(2,1)}, bf16[512,1024]{1,0:T(8,128)(2,1)}) async-done(((bf16[128,3072]{0,1:T(8,128)(2,1)}, bf16[128,1024]{1,0:T(8,128)(2,1)}, bf16[128,4096]{1,0:T(8,128)(2,1)}, bf16[512,1024]{1,0:T(8,128)(2,1)}), (bf16[128,3072]{0,1:T(8,128)(2,1)}, bf16[128,1024]{1,0:T(8,128)(2,1)}, ...) | async-done | bytes 3145744 | tf_op jit(solution)/shard_map/psum | solution.py:303
  (134 shorter events, 37.0 us)
Async XLA Ops:
  7.2 71.0 %all-gather.8.cloned.1.call-start = ((), (), s32[]{:S(2)}) async-start(), calls=%async_computation.8 | async-start | bytes 7077888 | tf_op jit(solution)/shard_map/all_gather | solution.py:233
  8.7 3.1 copy-start.20
  8.7 3.4 copy-start.21
  8.8 3.6 copy-start.22
  8.8 3.8 copy-start.23
  8.8 4.0 copy-start.24
  8.8 4.2 copy-start.19
  8.8 20.2 %copy-start = (bf16[1,384,1024]{2,1,0:T(8,128)(2,1)S(1)}, bf16[1,384,1024]{2,1,0:T(8,128)(2,1)}, u32[]{:S(2)}) copy-start(bf16[1,384,1024]{2,1,0:T(8,128)(2,1)} %param.14) | copy-start | bytes 2359300
  9.8 159.6 %all-gather.10.cloned.1.call-start = ((), (), s32[]{:S(2)}) async-start(), calls=%async_computation.9 | async-start | bytes 2359296 | tf_op jit(solution)/shard_map/all_gather | solution.py:235
  10.5 179.8 %all-gather.12.cloned.1.call-start = ((), (), s32[]{:S(2)}) async-start(), calls=%async_computation.10 | async-start | bytes 9437184 | tf_op jit(solution)/shard_map/all_gather | solution.py:236
  11.3 261.2 %all-gather.14.cloned.1.call-start = ((), (), s32[]{:S(2)}) async-start(), calls=%async_computation.11 | async-start | bytes 9437184 | tf_op jit(solution)/shard_map/all_gather | solution.py:237
  30.2 55.4 %copy-start.16 = (f32[1024]{0:T(1024)}, f32[1024]{0:T(1024)S(1)}, u32[]{:S(2)}) copy-start(f32[1024]{0:T(1024)S(1)} %get-tuple-element.80) | copy-start | bytes 12292
  87.2 4.6 copy-start.13
  87.2 5.1 copy-start.18
  87.2 50.4 %all-to-all-start = ((bf16[384,4,768]{2,0,1:T(8,128)(2,1)}), bf16[384,4,768]{2,0,1:T(8,128)(2,1)}, u32[]{:S(2)}, u32[]{:S(2)}) async-start(bf16[384,4,768]{2,0,1:T(8,128)(2,1)} %bitcast.136), calls=%async_computation | async-start | bytes 4718592 | tf_op jit(solution)/shard_map/all_to_all | solution.py:244
  162.3 16.1 %copy-start.1 = (bf16[1,384,1024]{2,1,0:T(8,128)(2,1)S(1)}, bf16[1,384,1024]{2,1,0:T(8,128)(2,1)}, u32[]{:S(2)}) copy-start(bf16[1,384,1024]{2,1,0:T(8,128)(2,1)} %param.14) | copy-start | bytes 2359300
  164.7 13.6 %all-to-all-start.1 = ((bf16[4,384,256]{1,2,0:T(8,128)(2,1)}), bf16[4,384,256]{1,2,0:T(8,128)(2,1)S(1)}, u32[]{:S(2)}, u32[]{:S(2)}) async-start(bf16[4,384,256]{1,2,0:T(8,128)(2,1)} %copy.61), calls=%async_computation.1 | async-start | bytes 1572864 | tf_op jit(solution)/shard_map/all_to_all | solution.py:246
  168.2 278.7 %reduce-scatter.5.cloned.1.call-start = ((), (), s32[]{:S(2)}) async-start(), calls=%async_computation.12 | async-start | bytes 7077888 | tf_op jit(solution)/shard_map/reduce_scatter | solution.py:278
  178.3 12.0 %copy-start.15 = (f32[1024]{0:T(1024)S(1)}, f32[1024]{0:T(1024)}, u32[]{:S(2)}) copy-start(f32[1024]{0:T(1024)} %get-tuple-element.79) | copy-start | bytes 12292
  190.4 82.1 %copy-start.9 = (bf16[1,384,1024]{2,1,0:T(8,128)(2,1)S(1)}, bf16[1,384,1024]{2,1,0:T(8,128)(2,1)}, u32[]{:S(2)}) copy-start(bf16[1,384,1024]{2,1,0:T(8,128)(2,1)} %param.27) | copy-start | bytes 2359300
  272.5 11.3 %copy-start.25 = (bf16[1024,4096]{1,0:T(8,128)(2,1)S(1)}, bf16[1024,4096]{1,0:T(8,128)(2,1)}, u32[]{:S(2)}) copy-start(bf16[1024,4096]{1,0:T(8,128)(2,1)} %all-gather.12.cloned.1.call-done) | copy-start | bytes 25165828
  283.8 3.9 copy-start.26
  283.8 3.9 copy-start.10
  341.4 32.5 %copy-start.2 = (bf16[1,384,1024]{2,1,0:T(8,128)(2,1)S(1)}, bf16[1,384,1024]{2,1,0:T(8,128)(2,1)}, u32[]{:S(2)}) copy-start(bf16[1,384,1024]{2,1,0:T(8,128)(2,1)} %param.14) | copy-start | bytes 2359300
  341.4 32.5 %copy-start.17 = (f32[1024]{0:T(1024)S(1)}, f32[1024]{0:T(1024)}, u32[]{:S(2)}) copy-start(f32[1024]{0:T(1024)} %copy-done.16) | copy-start | bytes 12292
  379.8 104.0 %reduce-scatter.7.cloned.1.call-start = ((), (), s32[]{:S(2)}) async-start(), calls=%async_computation.13 | async-start | bytes 2359296 | tf_op jit(solution)/shard_map/reduce_scatter | solution.py:273
  383.6 190.8 %reduce-scatter.9.cloned.1.call-start = ((), (), s32[]{:S(2)}) async-start(), calls=%async_computation.14 | async-start | bytes 9437184 | tf_op jit(solution)/shard_map/reduce_scatter | solution.py:272
  392.5 272.1 %reduce-scatter.11.cloned.1.call-start = ((), (), s32[]{:S(2)}) async-start(), calls=%async_computation.15 | async-start | bytes 9437184 | tf_op jit(solution)/shard_map/reduce_scatter | solution.py:271
  403.9 351.7 %all-reduce.4.cloned.1.call-start = ((), (), s32[]{:S(2)}) async-start(), calls=%async_computation.16 | async-start | bytes 6291456 | tf_op jit(solution)/shard_map/psum | solution.py:303
  449.1 215.5 %copy-start.14 = (f32[1024]{0:T(1024)S(1)}, f32[1024]{0:T(1024)}, u32[]{:S(2)}) copy-start(f32[1024]{0:T(1024)} %get-tuple-element.78) | copy-start | bytes 12292
  674.7 48.0 %copy-start.3 = (bf16[1,384,1024]{2,1,0:T(8,128)(2,1)S(1)}, bf16[1,384,1024]{2,1,0:T(8,128)(2,1)}, u32[]{:S(2)}) copy-start(bf16[1,384,1024]{2,1,0:T(8,128)(2,1)} %param.14) | copy-start | bytes 2359300
  755.5 3.5 copy-start.8
  (6 other events, 11.6 us)
Sparse Core Ops, SparseCore 0:
  10.2 67.9 all-gather.7
  79.8 27.2 all-gather.9
  108.7 81.6 all-gather.11
  191.8 80.6 all-gather.13
  379.9 66.8 reduce-scatter.4
  449.6 34.2 reduce-scatter.6
  486.1 88.1 reduce-scatter.8
  576.6 87.9 reduce-scatter.10
  668.6 86.8 all-reduce.3

commit v2 on v1

--- a/solution.py
+++ b/solution.py
@@ -82,28 +82,430 @@
     return (lane >= DH) if odd else (lane < DH)
 
 
-def attend_forward(tile, q_ref, k_ref, v_ref, qf_ref, kf_ref, out_ref, lse_ref):
-    length = k_ref.shape[0]
+MESH = pl.DeviceIdType.MESH
+
+
+class Place:
+    def __init__(self, fsdp_count):
+        self.depth = fsdp_count // 2
+        self.s = lax.axis_index("seq")
+        self.f = lax.axis_index("fsdp")
+        self.z = lax.div(self.f, 2)
+        self.c = lax.rem(self.f, 2)
+        self.s1 = self.s + 1 - 2 * lax.rem(self.s, 2)
+        self.s2 = self.s + 2 - 4 * lax.div(self.s, 2)
+        self.s3 = 3 - self.s
+        self.beside = (self.s, self.f + 1 - 2 * self.c)
+
+    def across(self, index):
+        return ((self.s1, self.s2, self.s3)[index], self.f)
+
+    def far(self, step):
+        return lax.rem(self.z + step, self.depth)
+
+    def back(self, step):
+        return lax.rem(self.z + self.depth - step, self.depth)
+
+    def along(self, z):
+        return (self.s, 2 * z + self.c)
+
+    def meet(self):
+        barrier = pltpu.get_barrier_semaphore()
+        peers = [self.beside] + [self.across(i) for i in range(3)]
+        for peer in peers:
+            pl.semaphore_signal(barrier, inc=1, device_id=peer, device_id_type=MESH)
+        self.each(1, self.depth, lambda step: pl.semaphore_signal(
+            barrier, inc=1, device_id=self.along(self.far(step)), device_id_type=MESH
+        ))
+        pl.semaphore_wait(barrier, len(peers) + self.depth - 1)
+
+    def each(self, start, stop, body):
+        if stop - start <= 8:
+            for step in range(start, stop):
+                body(step)
+        else:
+            lax.fori_loop(start, stop, lambda step, carry: (body(step), carry)[1], 0)
+
+
+def send(src, dst, sems, index, device):
+    sent, got = sems
+    return pltpu.make_async_remote_copy(
+        src_ref=src,
+        dst_ref=dst,
+        send_sem=sent.at[index],
+        recv_sem=got.at[index],
+        device_id=device,
+        device_id_type=MESH,
+    )
+
+
+def aligned(start, size):
+    return pl.ds(pl.multiple_of(start, size), size)
+
+
+class Gather:
+    def __init__(self, place, src, dst, split, sems):
+        self.place, self.src, self.dst, self.split = place, src, dst, split
+        self.rows, self.cols = src.shape
+        self.local, self.zs, self.xs, self.rs, self.cs = sems
+
+    def block(self, f, quarter=None, half=None):
+        rows = aligned(f * self.rows, self.rows)
+        if quarter is None:
+            return self.dst.at[rows]
+        wide = self.cols // 4
+        if half is None:
+            return self.dst.at[rows, aligned(quarter * wide, wide)]
+        return self.dst.at[rows, aligned(quarter * wide + half * (wide // 2), wide // 2)]
+
+    def own_copy(self):
+        return pltpu.make_async_copy(self.src, self.block(self.place.f), self.local)
+
+    def core_copy(self, step):
+        p = self.place
+        f = 2 * p.far(step) + p.c
+        src = self.src if isinstance(step, int) and step == 0 else self.block(f)
+        return send(src, self.block(f), self.cs, step, p.beside)
+
+    def core_arrival(self, step):
+        p = self.place
+        there = self.block(2 * p.far(step) + 1 - p.c)
+        return send(there, there, self.cs, step, p.beside)
+
+    def z_copy(self, step):
+        p = self.place
+        if self.split:
+            wide = self.cols // 4
+            src, dst = self.src.at[:, aligned(p.s * wide, wide)], self.block(p.f, p.s)
+        else:
+            src, dst = self.src, self.block(p.f)
+        return send(src, dst, self.zs, step, p.along(p.back(step)))
+
+    def z_arrival(self, step):
+        p = self.place
+        f = 2 * p.far(step) + p.c
+        there = self.block(f, p.s) if self.split else self.block(f)
+        return send(there, there, self.zs, step, p.along(p.far(step)))
+
+    def x_copy(self, step, way):
+        p = self.place
+        there = self.block(2 * p.far(step) + p.c, p.s)
+        return send(there, there, self.xs[way], step, p.across(way))
+
+    def x_arrival(self, step, way):
+        p = self.place
+        there = self.block(2 * p.far(step) + p.c, (p.s1, p.s2)[way])
+        return send(there, there, self.xs[way], step, p.across(way))
+
+    def relay_copy(self, step, way):
+        p = self.place
+        there = self.block(2 * p.far(step) + p.c, (p.s2, p.s1)[way], 1 - way)
+        return send(there, there, self.rs[way], step, p.across(way))
+
+    def relay_arrival(self, step, way):
+        p = self.place
+        there = self.block(2 * p.far(step) + p.c, p.s3, 1 - way)
+        return send(there, there, self.rs[way], step, p.across(way))
+
+    def begin(self):
+        self.place.each(1, self.place.depth, lambda step: self.z_copy(step).start())
+        self.own_copy().start()
+        self.core_copy(0).start()
+
+    def swap(self, step):
+        self.z_arrival(step).wait_recv()
+        if self.split:
+            for way in (0, 1):
+                self.x_copy(step, way).start()
+        else:
+            self.core_copy(step).start()
+
+    def relay(self, step):
+        if self.split:
+            for way in (0, 1):
+                self.x_arrival(step, way).wait_recv()
+            for way in (0, 1):
+                self.relay_copy(step, way).start()
+
+    def share(self, step):
+        if self.split:
+            for way in (0, 1):
+                self.relay_arrival(step, way).wait_recv()
+            self.core_copy(step).start()
+
+    def finish(self):
+        self.own_copy().wait()
+        self.core_copy(0).wait_send()
+        self.core_arrival(0).wait_recv()
+
+        def close(step):
+            self.z_copy(step).wait_send()
+            if self.split:
+                for way in (0, 1):
+                    self.x_copy(step, way).wait_send()
+                    self.relay_copy(step, way).wait_send()
+            self.core_copy(step).wait_send()
+            self.core_arrival(step).wait_recv()
+
+        self.place.each(1, self.place.depth, close)
+
+    @staticmethod
+    def scratch(depth):
+        pair = [pltpu.SemaphoreType.DMA((depth,))] * 2
+        return [pltpu.SemaphoreType.DMA] + pair * 6
+
+    @staticmethod
+    def take(refs):
+        pairs = [(refs[i], refs[i + 1]) for i in range(1, 13, 2)]
+        return (refs[0], pairs[0], pairs[1:3], pairs[3:5], pairs[5])
+
+
+GATHER_SEMS = 13
+
+
+def gather_steps(place, gathers, between):
+    depth = place.depth
+    work = list(between)
+
+    def stage(step, swap, relay, share):
+        for one in gathers:
+            if swap:
+                one.swap(step)
+        for one in gathers:
+            if relay:
+                one.relay(step - 1)
+        for one in gathers:
+            if share:
+                one.share(step - 2)
+
+    if depth <= 8:
+        for step in range(1, depth + 2):
+            stage(step, step < depth, 2 <= step <= depth, step >= 3)
+            if work:
+                work.pop(0)()
+    else:
+        stage(1, True, False, False)
+        stage(2, True, True, False)
+        lax.fori_loop(3, depth, lambda step, carry: (stage(step, True, True, True), carry)[1], 0)
+        stage(depth, False, True, True)
+        stage(depth + 1, False, False, True)
+    for rest in work:
+        rest()
+
+
+def first_gather_kernel(fsdp_count, w_ref, vec_ref, seg_ref, w_all, vec_all, seg_all, *sems):
+    place = Place(fsdp_count)
+    weight = Gather(place, w_ref, w_all, True, Gather.take(sems[:GATHER_SEMS]))
+    vector = Gather(place, vec_ref, vec_all, False, Gather.take(sems[GATHER_SEMS : 2 * GATHER_SEMS]))
+    local, sent, got = sems[2 * GATHER_SEMS :]
+    rows = seg_ref.shape[0]
+    place.meet()
+    weight.begin()
+    vector.begin()
+    own = pltpu.make_async_copy(seg_ref, seg_all.at[aligned(place.s * rows, rows)], local)
+    own.start()
+    for way in range(3):
+        send(seg_ref, seg_all.at[aligned(place.s * rows, rows)], (sent, got), way, place.across(way)).start()
+    gather_steps(place, [vector, weight], [])
+    own.wait()
+    for way in range(3):
+        there = seg_all.at[aligned((place.s1, place.s2, place.s3)[way] * rows, rows)]
+        arrival = send(there, there, (sent, got), way, place.across(way))
+        arrival.wait_recv()
+        send(seg_ref, seg_all.at[aligned(place.s * rows, rows)], (sent, got), way, place.across(way)).wait_send()
+    vector.finish()
+    weight.finish()
+
+
+def first_gather(fsdp_count, w_shard, vec, seg):
+    anywhere = pl.BlockSpec(memory_space=pl.ANY)
+    return pl.pallas_call(
+        functools.partial(first_gather_kernel, fsdp_count),
+        out_shape=(
+            jax.ShapeDtypeStruct((fsdp_count * w_shard.shape[0], w_shard.shape[1]), w_shard.dtype),
+            jax.ShapeDtypeStruct((fsdp_count * vec.shape[0], vec.shape[1]), vec.dtype),
+            jax.ShapeDtypeStruct((4 * seg.shape[0], seg.shape[1]), seg.dtype),
+        ),
+        in_specs=[anywhere] * 3,
+        out_specs=(anywhere,) * 3,
+        scratch_shapes=Gather.scratch(fsdp_count // 2) * 2
+        + [pltpu.SemaphoreType.DMA, pltpu.SemaphoreType.DMA((3,)), pltpu.SemaphoreType.DMA((3,))],
+        compiler_params=pltpu.CompilerParams(collective_id=1, has_side_effects=True),
+    )(w_shard, vec, seg)
+
+
+def attend_unit(pair, odd, tile, heads_ref, qf_ref, kf_ref, keys_sc, values_t, out_ref, lse_ref):
+    length = heads_ref.shape[0]
+    third = heads_ref.shape[1] // 3
     scale = jnp.asarray(1.0 / math.sqrt(DH), BF16)
-    values_t = v_ref[...].T
-    for odd in (0, 1):
-        mine = own_lanes(odd, (length, LANES))
-        keys = jnp.where(mine, k_ref[...], kf_ref[...])
-        for start in range(0, length, tile):
-            rows = pl.ds(start, tile)
-            lanes = own_lanes(odd, (tile, LANES))
-            queries = jnp.where(lanes, q_ref[rows, :] * scale, qf_ref[odd, rows, :])
-            scores = dot_nt(keys, queries)
-            top = jnp.max(scores, axis=0, keepdims=True)
-            prob = jnp.exp(scores - top)
-            total = jnp.sum(prob, axis=0, keepdims=True)
-            mixed = dot_nn(values_t, prob.astype(BF16)) / total
-            lse_ref[0, odd, rows] = (top + jnp.log(total))[0]
-            result = mixed.T.astype(BF16)
-            if odd:
-                out_ref[rows, :] = jnp.where(lanes, result, out_ref[rows, :])
-            else:
-                out_ref[rows, :] = result
+    cols = pl.ds(pair * LANES, LANES)
+    if not odd:
+        values_t[...] = heads_ref[:, pl.ds(2 * third + pair * LANES, LANES)].T
+    mine = own_lanes(odd, (length, LANES))
+    keys_sc[...] = jnp.where(mine, heads_ref[:, pl.ds(third + pair * LANES, LANES)], kf_ref[...])
+
+    def one_tile(index, carry):
+        rows = aligned(index * tile, tile)
+        lanes = own_lanes(odd, (tile, LANES))
+        queries = jnp.where(lanes, heads_ref[rows, cols] * scale, qf_ref[2 * pair + odd, rows, :])
+        scores = dot_nt(keys_sc[...], queries)
+        top = jnp.max(scores, axis=0, keepdims=True)
+        prob = jnp.exp(scores - top)
+        total = jnp.sum(prob, axis=0, keepdims=True)
+        mixed = dot_nn(values_t[...], prob.astype(BF16)) / total
+        lse_ref[pair, pl.ds(odd, 1), rows] = top + jnp.log(total)
+        result = mixed.T.astype(BF16)
+        if odd:
+            out_ref[rows, cols] = jnp.where(lanes, result, out_ref[rows, cols])
+        else:
+            out_ref[rows, cols] = result
+        return carry
+
+    lax.fori_loop(0, length // tile, one_tile, 0, unroll=2)
+
+
+def forward_kernel(
+    fsdp_count,
+    qkv_ref,
+    qf_ref,
+    kf_ref,
+    out_w_ref,
+    down_w_ref,
+    in_w_ref,
+    heads_all,
+    lse_ref,
+    att_all,
+    out_w_all,
+    down_w_all,
+    in_w_all,
+    heads_sc,
+    att_sc,
+    keys_sc,
+    values_t,
+    *sems,
+):
+    place = Place(fsdp_count)
+    rows, width = qkv_ref.shape[0], heads_sc.shape[1]
+    gathers = [
+        Gather(place, src, dst, True, Gather.take(sems[i * GATHER_SEMS : (i + 1) * GATHER_SEMS]))
+        for i, (src, dst) in enumerate(
+            ((out_w_ref, out_w_all), (in_w_ref, in_w_all), (down_w_ref, down_w_all))
+        )
+    ]
+    own_sem, q_sent, q_got, copy_sem, a_sent, a_got, a_own = sems[3 * GATHER_SEMS :]
+    seats = (place.s1, place.s2, place.s3)
+
+    def part(seat):
+        return qkv_ref.at[:, aligned(seat * width, width)]
+
+    def slot(seat):
+        return heads_sc.at[aligned(seat * rows, rows)]
+
+    place.meet()
+    for way in range(3):
+        send(part(seats[way]), slot(place.s), (q_sent, q_got), way, place.across(way)).start()
+    own = pltpu.make_async_copy(part(place.s), slot(place.s), own_sem)
+    own.start()
+    for one in gathers:
+        one.begin()
+    own.wait()
+    for way in range(3):
+        send(slot(seats[way]), slot(seats[way]), (q_sent, q_got), way, place.across(way)).wait_recv()
+    keep = pltpu.make_async_copy(heads_sc, heads_all, copy_sem)
+    keep.start()
+
+    pairs = att_sc.shape[1] // LANES
+
+    def att_copy(pair, way):
+        cols = aligned((place.s * pairs + pair) * LANES, LANES)
+        return send(
+            att_sc.at[aligned(seats[way] * rows, rows), pl.ds(pair * LANES, LANES)],
+            att_all.at[:, cols],
+            (a_sent, a_got),
+            pair * 3 + way,
+            place.across(way),
+        )
+
+    def att_own(pair):
+        cols = aligned((place.s * pairs + pair) * LANES, LANES)
+        return pltpu.make_async_copy(
+            att_sc.at[aligned(place.s * rows, rows), pl.ds(pair * LANES, LANES)],
+            att_all.at[:, cols],
+            a_own.at[pair],
+        )
+
+    def att_arrival(pair, way):
+        there = att_all.at[:, aligned((seats[way] * pairs + pair) * LANES, LANES)]
+        return send(there, there, (a_sent, a_got), pair * 3 + way, place.across(way))
+
+    def unit(pair, odd):
+        attend_unit(pair, odd, 256, heads_sc, qf_ref, kf_ref, keys_sc, values_t, att_sc, lse_ref)
+        if odd:
+            for way in range(3):
+                att_copy(pair, way).start()
+            att_own(pair).start()
+
+    gather_steps(
+        place,
+        gathers,
+        [functools.partial(unit, pair, odd) for pair in range(pairs) for odd in (0, 1)],
+    )
+    keep.wait()
+    for way in range(3):
+        send(part(seats[way]), slot(place.s), (q_sent, q_got), way, place.across(way)).wait_send()
+        for pair in range(pairs):
+            att_copy(pair, way).wait_send()
+            att_arrival(pair, way).wait_recv()
+    for pair in range(pairs):
+        att_own(pair).wait()
+    for one in gathers:
+        one.finish()
+
+
+def forward_attention(fsdp_count, qkv_rows, query_feats, key_feats, w_out, w_down, w_in):
+    rows, width = qkv_rows.shape
+    length = 4 * rows
+    heads = query_feats.shape[0]
+    pairs = heads // 2
+    depth = fsdp_count // 2
+    anywhere = pl.BlockSpec(memory_space=pl.ANY)
+    vmem = pl.BlockSpec(memory_space=pltpu.VMEM)
+
+    def whole(shard):
+        return jax.ShapeDtypeStruct((fsdp_count * shard.shape[0], shard.shape[1]), shard.dtype)
+
+    return pl.pallas_call(
+        functools.partial(forward_kernel, fsdp_count),
+        out_shape=(
+            jax.ShapeDtypeStruct((length, width // 4), BF16),
+            jax.ShapeDtypeStruct((pairs, 2, length), F32),
+            jax.ShapeDtypeStruct((rows, width // 3), BF16),
+            whole(w_out),
+            whole(w_down),
+            whole(w_in),
+        ),
+        in_specs=[anywhere, vmem, vmem, anywhere, anywhere, anywhere],
+        out_specs=(anywhere, vmem, anywhere, anywhere, anywhere, anywhere),
+        scratch_shapes=[
+            pltpu.VMEM((length, width // 4), BF16),
+            pltpu.VMEM((length, heads * DH), BF16),
+            pltpu.VMEM((length, LANES), BF16),
+            pltpu.VMEM((LANES, length), BF16),
+        ]
+        + Gather.scratch(depth) * 3
+        + [
+            pltpu.SemaphoreType.DMA,
+            pltpu.SemaphoreType.DMA((3,)),
+            pltpu.SemaphoreType.DMA((3,)),
+            pltpu.SemaphoreType.DMA,
+            pltpu.SemaphoreType.DMA((3 * pairs,)),
+            pltpu.SemaphoreType.DMA((3 * pairs,)),
+            pltpu.SemaphoreType.DMA((pairs,)),
+        ],
+        compiler_params=pltpu.CompilerParams(
+            collective_id=2, has_side_effects=True, vmem_limit_bytes=40 << 20
+        ),
+    )(qkv_rows, query_feats, key_feats, w_out, w_down, w_in)
 
 
 def attend_backward(
@@ -142,35 +544,6 @@
     return pl.BlockSpec((length, LANES), lambda p: (0, p + offset))
 
 
-def attention_forward(by_heads, query_feats, key_feats):
-    length = by_heads.shape[0]
-    heads = query_feats.shape[0]
-    pairs = heads // 2
-    return pl.pallas_call(
-        functools.partial(attend_forward, 256),
-        grid=(pairs,),
-        out_shape=(
-            jax.ShapeDtypeStruct((length, heads * DH), BF16),
-            jax.ShapeDtypeStruct((pairs, 2, length), F32),
-        ),
-        in_specs=[
-            column_spec(length, 0),
-            column_spec(length, pairs),
-            column_spec(length, 2 * pairs),
-            pl.BlockSpec((2, length, LANES), lambda p: (p, 0, 0)),
-            pl.BlockSpec((length, LANES), lambda p: (0, 0)),
-        ],
-        out_specs=(
-            column_spec(length, 0),
-            pl.BlockSpec((1, 2, length), lambda p: (p, 0, 0)),
-        ),
-        compiler_params=pltpu.CompilerParams(vmem_limit_bytes=56 << 20),
-        cost_estimate=pl.CostEstimate(
-            flops=heads * length * length * 512, bytes_accessed=8 << 20, transcendentals=heads * length * length
-        ),
-    )(by_heads, by_heads, by_heads, query_feats, key_feats)
-
-
 def attention_backward(by_heads, query_feats, key_feats, grad_out, lse):
     length = by_heads.shape[0]
     heads = query_feats.shape[0]
@@ -221,29 +594,30 @@
     b_down,
     cotangent,
 ):
-    gather = functools.partial(lax.all_gather, axis_name="fsdp", axis=0, tiled=True)
     width = w_qkv.shape[1] // 3
     share = ln1_gain.shape[0]
-    packed = jnp.concatenate([ln1_gain, ln1_bias, ln2_gain, ln2_bias, b_down, b_in])[None]
-    packed = gather(packed).astype(F32)
+    packed = jnp.concatenate([ln1_gain, ln1_bias, ln2_gain, ln2_bias, b_down, b_in])
+    packed_rows = -(-packed.shape[0] // (16 * LANES)) * 16
+    packed = jnp.pad(packed, (0, packed_rows * LANES - packed.shape[0])).reshape(packed_rows, LANES)
+    tok_count = segment_ids.shape[1]
+    seg_rows = -(-tok_count // (8 * LANES)) * 8
+    seg = jnp.pad(segment_ids[0], (0, seg_rows * LANES - tok_count)).reshape(seg_rows, LANES)
+    qkv_weight, packed, seg = first_gather(fsdp_count, swap_thirds(w_qkv, 3, seq_count), packed, seg)
+    packed = packed.reshape(fsdp_count, packed_rows * LANES).astype(F32)
     gain_one, bias_one, gain_two, bias_two, down_bias = (
         packed[:, i * share : (i + 1) * share].reshape(-1) for i in range(5)
     )
-    in_bias = packed[:, 5 * share :].reshape(-1)
-    qkv_weight = gather(swap_thirds(w_qkv, 3, seq_count))
-    seq_ids = lax.all_gather(segment_ids[0], "seq", axis=0, tiled=True)
-    out_weight = gather(w_out)
-    in_weight = gather(w_in)
-    down_weight = gather(w_down)
+    in_bias = packed[:, 5 * share : 5 * share + b_in.shape[0]].reshape(-1)
+    seq_ids = seg.reshape(seq_count, seg_rows * LANES)[:, :tok_count].reshape(-1)
     query_feats, key_feats = mask_features(random_blocks, seq_ids, 6)
 
     token_rows = tokens[0].astype(F32)
     hat_one, inv_one = layer_norm_parts(token_rows)
     normed_one = (hat_one * gain_one + bias_one).astype(BF16)
     qkv_rows = dot_nn(normed_one, qkv_weight).astype(BF16)
-    by_heads = lax.all_to_all(qkv_rows, "seq", split_axis=1, concat_axis=0, tiled=True)
-    att_heads, lse = attention_forward(by_heads, query_feats, key_feats)
-    att_rows = lax.all_to_all(att_heads, "seq", split_axis=0, concat_axis=1, tiled=True)
+    by_heads, lse, att_rows, out_weight, down_weight, in_weight = forward_attention(
+        fsdp_count, qkv_rows, query_feats, key_feats, w_out, w_down, w_in
+    )
     hidden = token_rows + dot_nn(att_rows, out_weight)
     hat_two, inv_two = layer_norm_parts(hidden)
     normed_two = (hat_two * gain_two + bias_two).astype(BF16)

time: 775 us -> 725 us (0.935)
  waiting for transfers between devices: 427 us -> 295 us
  Pallas kernels: 52.6 us -> 182 us
  blocking collectives: 132 us -> 91.9 us
  starting transfers between devices: 9.14 us -> 0.46 us
    all_gather x4 -> x0, waiting for transfers between devices: 130 us -> none  [the longest x1 73.1 us: per_device(): down_weight = gather(w_down)]
    pallas_call x1 -> x2, Pallas kernels: 24.7 us -> 154 us  [the longest x1 109 us: forward_attention(): pl.pallas_call(functools.partial(forward_kernel, fsdp_count), out_shape=(...]
    all_gather x2 -> x0, blocking collectives: 46.8 us -> none  [the longest x1 31 us: per_device(): seq_ids = lax.all_gather(segment_ids[0], 'seq', axis=0, tiled=True)]
    all_to_all x2 -> x0, waiting for transfers between devices: 8.96 us -> none  [the longest x1 8.95 us: per_device(): lax.all_to_all(att_heads, 'seq', split_axis=0, concat_axis=1, tiled=True)]
    all_to_all x2 -> x0, starting transfers between devices: 8.12 us -> none  [the longest x1 4.62 us: per_device(): lax.all_to_all(qkv_rows, 'seq', split_axis=1, concat_axis=0, tiled=True)]
  transfers between devices with their start and end apart: 11 -> 5, of which waited for: 9 -> 5; matrix products, arithmetic and copies ran while one was open for 12% -> 7% of each run, Pallas kernels for 3% -> 0%
where the time goes in v2:
time: 725 us; the launch traced here: 716 us
  waiting for transfers between devices  295 us (41%)
  Pallas kernels  182 us (25%)
  blocking collectives  91.9 us (13%)
  matrix products  79.5 us (11%)
  local copies, waits for them, and re-layouts  37.6 us (5%)
  between operations  14.8 us (2%)
  other arithmetic  13.9 us (2%)
    pallas_call x1, Pallas kernels, forward_attention(): pl.pallas_call(functools.partial(forward_kernel, fsdp_count), out_shape=(...  109 us
    reduce_scatter x1, waiting for transfers between devices, per_device(): share_in = scatter(dot_tn(normed_two, grad_pre).astype(BF16))  90.6 us
    reduce_scatter x1, waiting for transfers between devices, per_device(): share_down = scatter(dot_tn(act_low, cot_low).astype(BF16))  90.2 us
    reduce_scatter x1, waiting for transfers between devices, per_device(): share_qkv = scatter(dot_tn(normed_one, grad_qkv_rows).astype(BF16))  50 us
    pallas_call x1, Pallas kernels, first_gather(): pl.pallas_call(functools.partial(first_gather_kernel, fsdp_count), out_sh...  45.1 us
    psum x1, blocking collectives, per_device(): small = lax.psum(small, ('seq', 'fsdp'))  38.4 us
    reduce_scatter x1, waiting for transfers between devices, per_device(): share_out = scatter(dot_tn(att_rows, hidden_low).astype(BF16))  34.6 us
    all_to_all x1, blocking collectives, per_device(): lax.all_to_all(grad_heads, 'seq', split_axis=0, concat_axis=1, tiled=True)  31.1 us
  transfers between devices with their start and end apart: 5, of which 5 were waited for; matrix products, arithmetic and copies ran while one was open for 7% of the time, Pallas kernels for 0%

profile of v2, /device:TPU:0, one launch (start us, length us, event | category | flops | bytes accessed | tf_op | source)
XLA Modules:
  0.0 715.5 jit_solution(15132852378546129500)
XLA Ops:
  7.3 1.5 copy.44
  12.6 45.1 %shard_map.229 = (bf16[1024,3072]{1,0:T(8,128)(2,1)}, bf16[128,128]{1,0:T(8,128)(2,1)}, s32[32,128]{1,0:T(8,128)}) custom-call(bf16[128,3072]{1,0:T(8,128)(2,1)} %copy.46.w_ref, bf16[16,128]{1,0:T(8,128)(2,1)} %pad_bitcast_fusion.1.vec_ref, s32[8,128]{1,0:T(8,128)} %pad_bitcast_fusion.seg_ref), custom_call_target="tpu_custom_call" | custom-call | tf_op jit(solution)/shard_map/pallas_call | solution.py:322
  66.4 9.5 %concatenate.20.qf_ref = bf16[4,1536,128]{2,1,0:T(8,128)(2,1)S(1)} concatenate(bf16[4,1536,24]{2,1,0:T(8,128)(2,1)S(1)} %bitcast.140, bf16[4,1536,6]{2,1,0:T(8,128)(2,1)} %broadcast_in_dim.61, bf16[4,1536,34]{2,1,0:T(8,128)(2,1)} %broadcast_in_dim.62, bf16[4,1536,24]{2,1,0:T(8,128)(2,1)S(1)} %bitcast.141, bf16[4,1536,6]{2,1,0:T(8,128)(2,1)} %broadcast_in_dim.61, ...), dimensions={2} | concatenate | bytes 3145728 | tf_op jit(solution)/shard_map/concatenate | solution.py:75
  76.1 3.4 concatenate.21.kf_ref
  79.6 6.0 convolution_convert_fusion.3.qkv_ref
  85.6 108.8 %shard_map.230 = (bf16[1536,768]{1,0:T(8,128)(2,1)S(1)}, f32[2,2,1536]{2,1,0:T(2,128)S(1)}, bf16[384,1024]{1,0:T(8,128)(2,1)S(1)}, bf16[1024,1024]{1,0:T(8,128)(...) custom-call(bf16[384,3072]{1,0:T(8,128)(2,1)S(1)} %convolution_convert_fusion.3.qkv_ref, ...), custom_call_target="tpu_custom_call" | custom-call | tf_op jit(solution)/shard_map/pallas_call | solution.py:477
  196.3 9.8 %convolution_add_fusion = f32[384,4096]{1,0:T(8,128)} fusion(bf16[1024,4096]{1,0:T(8,128)(2,1)} %get-tuple-element.29, f32[4096]{0:T(1024)S(1)} %bitcast.152, f32[384,1024]{1,0:T(8,128)S(1)} %get-tuple-element.87, f32[1024]{0:T(1024)S(1)} %copy-done.19, f32[1024]{0:T(1024)S(1)} %get-tuple-element.74, f32[384]{0:T(512)S(1)} %add_rsqrt_fusion, ...), kind=kOutput, calls=%fused_computation.20 | convolution fusion | flops 3224764416 | bytes 16280576 | tf_op jit(solution)/shard_map/dot_general | solution.py:35
  206.1 10.2 %convert_reduce_fusion = (f32[4096]{0:T(1024)S(1)}, bf16[384,4096]{1,0:T(8,128)(2,1)S(1)}) fusion(f32[384,4096]{1,0:T(8,128)} %convolution_add_fusion, bf16[4096,1024]{1,0:T(8,128)(2,1)S(1)} %bitcast.155, bf16[1,384,1024]{2,1,0:T(8,128)(2,1)S(1)} %copy-done.13), kind=kOutput, calls=%fused_computation.17 | convolution fusion | flops 3262115840 | bytes 18628608 | tf_op jit(solution)/shard_map/dot_general | solution.py:39
  216.3 3.9 multiply_reduce_fusion
  221.9 22.4 %all_to_all.38 = bf16[384,4,256]{2,0,1:T(8,128)(2,1)} all-to-all(bf16[384,4,256]{2,0,1:T(8,128)(2,1)S(1)} %bitcast.144), channel_id=1, replica_groups=mesh['seq'=4,'fsdp'=8] {'seq'}, dimensions={1} | all-to-all | bytes 1572864 | tf_op jit(solution)/shard_map/all_to_all | solution.py:641
  244.4 27.9 %shard_map.231 = (bf16[1536,256]{1,0:T(8,128)(2,1)}, bf16[1536,256]{1,0:T(8,128)(2,1)}, bf16[1536,256]{1,0:T(8,128)(2,1)}) custom-call(bf16[1536,768]{1,0:T(8,128)(2,1)} %copy-done.5, bf16[1536,768]{1,0:T(8,128)(2,1)} %copy-done.5, bf16[1536,768]{1,0:T(8,128)(2,1)} %copy-done.5, bf16[4,1536,128]{2,1,0:T(8,128)(2,1)} %copy-done, bf16[1536,128]{1,0:T(8,128)(2,1)} %copy-done.1, ...), custom_call_target="tpu_custom_call" | custom-call | flops 12079595520 | bytes 12582912 | tf_op jit(solution)/shard_map/pallas_call | solution.py:552
  272.3 3.2 pad_maximum_fusion
  275.5 4.3 copy.50
  279.8 31.1 %all_to_all.39 = bf16[4,384,768]{1,2,0:T(8,128)(2,1)S(1)} all-to-all(bf16[4,384,768]{1,2,0:T(8,128)(2,1)} %copy.50), channel_id=1, replica_groups=mesh['seq'=4,'fsdp'=8] {'seq'}, dimensions={0} | all-to-all | bytes 4718592 | tf_op jit(solution)/shard_map/all_to_all | solution.py:651
  310.9 1.4 copy-done.10
  312.3 5.9 convolution_convert_fusion.2
  318.3 2.6 convolution_convert_fusion.4
  321.0 10.4 %convolution_convert_fusion.1 = bf16[1024,4096]{1,0:T(8,128)(2,1)} fusion(bf16[384,4096]{1,0:T(8,128)(2,1)} %copy-done.29, f32[384,1024]{1,0:T(8,128)} %copy-done.9, f32[1024]{0:T(1024)S(1)} %copy-done.19, f32[1024]{0:T(1024)S(1)} %get-tuple-element.74, f32[384]{0:T(512)S(1)} %add_rsqrt_fusion, f32[384]{0:T(512)S(1)} %broadcast_multiply_fusion.4), kind=kOutput, calls=%fused_computation.5 | convolution fusion | flops 3227385856 | bytes 13118464 | tf_op jit(solution)/shard_map/dot_general | solution.py:43
  332.5 10.5 %convolution_convert_fusion = bf16[4096,1024]{1,0:T(8,128)(2,1)} fusion(bf16[1,384,1024]{2,1,0:T(8,128)(2,1)S(1)} %copy-done.14, f32[384,4096]{1,0:T(8,128)} %convolution_add_fusion), kind=kOutput, calls=%fused_computation.4 | convolution fusion | flops 3239575552 | bytes 15466496 | tf_op jit(solution)/shard_map/dot_general | solution.py:43
  343.4 50.0 %reduce-scatter.5.cloned.1.call-done = bf16[128,3072]{1,0:T(8,128)(2,1)} async-done(((bf16[1024,3072]{1,0:T(8,128)(2,1)}), bf16[128,3072]{1,0:T(8,128)(2,1)}) %reduce-scatter.5.cloned.1.call-update) | async-done | bytes 786448 | tf_op jit(solution)/shard_map/reduce_scatter | solution.py:652
  393.4 1.5 copy.51
  395.8 34.6 %reduce-scatter.7.cloned.1.call-done = bf16[128,1024]{1,0:T(8,128)(2,1)} async-done(((bf16[1024,1024]{1,0:T(8,128)(2,1)}), bf16[128,1024]{1,0:T(8,128)(2,1)}) %reduce-scatter.7.cloned.1.call-update) | async-done | bytes 262160 | tf_op jit(solution)/shard_map/reduce_scatter | solution.py:647
  430.4 90.6 %reduce-scatter.9.cloned.1.call-done = bf16[128,4096]{1,0:T(8,128)(2,1)} async-done(((bf16[1024,4096]{1,0:T(8,128)(2,1)}), bf16[128,4096]{1,0:T(8,128)(2,1)}) %reduce-scatter.9.cloned.1.call-update) | async-done | bytes 1048592 | tf_op jit(solution)/shard_map/reduce_scatter | solution.py:646
  521.1 90.2 %reduce-scatter.11.cloned.1.call-done = bf16[512,1024]{1,0:T(8,128)(2,1)} async-done(((bf16[4096,1024]{1,0:T(8,128)(2,1)}), bf16[512,1024]{1,0:T(8,128)(2,1)}) %reduce-scatter.11.cloned.1.call-update) | async-done | bytes 1048592 | tf_op jit(solution)/shard_map/reduce_scatter | solution.py:645
  611.3 10.4 %fusion.30 = bf16[1,384,1024]{2,1,0:T(8,128)(2,1)} fusion(f32[384,1024]{1,0:T(8,128)} %copy-done.9, bf16[4096,1024]{1,0:T(8,128)(2,1)} %get-tuple-element.30, f32[1024]{0:T(1024)S(1)} %copy-done.18, f32[384,4096]{1,0:T(8,128)} %convolution_add_fusion), kind=kOutput, calls=%fused_computation.59 | convolution fusion | flops 3236560896 | bytes 17043456 | tf_op jit(solution)/shard_map/dot_general | solution.py:35
  621.7 7.6 %fusion.24 = (f32[1024]{0:T(1024)S(1)}, f32[384]{0:T(512)S(1)}, f32[384]{0:T(512)S(1)}, f32[1024]{0:T(1024)S(1)}, f32[384,1024]{1,0:T(8,128)}) fusion(bf16[1,384,1024]{2,1,0:T(8,128)(2,1)S(1)} %copy-done.8, f32[384]{0:T(512)S(1)} %add_rsqrt_fusion.1, f32[384]{0:T(512)S(1)} %broadcast_multiply_fusion.5, f32[1024]{0:T(1024)S(1)} %get-tuple-element.78, ...), kind=kOutput, calls=%fused_computation.44 | convolution fusion | flops 2419848192 | bytes 11028480 | tf_op jit(solution)/shard_map/dot_general | solution.py:39
  629.4 38.4 %psum.35 = f32[8,1152]{1,0:T(8,128)S(1)} all-reduce(f32[8,1152]{1,0:T(8,128)S(1)} %constant_dynamic-update-slice_fusion), channel_id=1, replica_groups=mesh['seq'=4,'fsdp'=8] {'seq','fsdp'}, use_global_device_ids=true, to_apply=%region_15.16 | all-reduce | flops 9216 | bytes 73728 | tf_op jit(solution)/shard_map/psum | solution.py:674
  669.1 2.9 fusion.33
  671.9 30.0 %all-reduce.6.cloned.1.call-done = (bf16[128,3072]{0,1:T(8,128)(2,1)}, bf16[128,1024]{1,0:T(8,128)(2,1)}, bf16[128,4096]{1,0:T(8,128)(2,1)}, bf16[512,1024]{1,0:T(8,128)(2,1)}) async-done(((bf16[128,3072]{0,1:T(8,128)(2,1)}, bf16[128,1024]{1,0:T(8,128)(2,1)}, bf16[128,4096]{1,0:T(8,128)(2,1)}, bf16[512,1024]{1,0:T(8,128)(2,1)}), (bf16[128,3072]{0,1:T(8,128)(2,1)}, bf16[128,1024]{1,0:T(8,128)(2,1)}, ...) | async-done | bytes 3145744 | tf_op jit(solution)/shard_map/psum | solution.py:677
  702.0 2.7 copy.53
  705.5 1.5 convert_element_type.131
  707.0 1.6 convert_element_type.133
  (136 shorter events, 20.7 us)
Async XLA Ops:
  7.2 386.2 %reduce-scatter.5.cloned.1.call-start = ((), (), s32[]{:S(2)}) async-start(), calls=%async_computation.6 | async-start | bytes 7077888 | tf_op jit(solution)/shard_map/reduce_scatter | solution.py:652
  7.3 2.9 copy-start.24
  7.3 3.0 copy-start.25
  7.3 3.3 copy-start.26
  7.3 3.5 copy-start.27
  7.3 3.7 copy-start.28
  7.3 3.9 copy-start.23
  7.3 4.7 copy-start.22
  8.9 50.3 %copy-start.7 = (bf16[1,384,1024]{2,1,0:T(8,128)(2,1)S(1)}, bf16[1,384,1024]{2,1,0:T(8,128)(2,1)}, u32[]{:S(2)}) copy-start(bf16[1,384,1024]{2,1,0:T(8,128)(2,1)} %param.14) | copy-start | bytes 2359300
  9.0 50.8 %copy-start.17 = (s32[4,22,3]{1,0,2:T(4,128)S(1)}, s32[4,22,3]{1,0,2:T(4,128)}, u32[]{:S(2)}) copy-start(s32[4,22,3]{1,0,2:T(4,128)} %param.16) | copy-start | bytes 3172
  76.0 9.6 %copy-start = (bf16[4,1536,128]{2,1,0:T(8,128)(2,1)}, bf16[4,1536,128]{2,1,0:T(8,128)(2,1)S(1)}, u32[]{:S(2)}) copy-start(bf16[4,1536,128]{2,1,0:T(8,128)(2,1)S(1)} %concatenate.20.qf_ref) | copy-start | bytes 4718596
  76.0 3.5 copy-start.8
  76.0 3.5 copy-start.20
  79.5 6.1 copy-start.1
  79.5 6.1 copy-start.2
  79.5 6.1 copy-start.3
  79.5 6.1 copy-start.4
  195.9 24.2 %copy-start.9 = (f32[384,1024]{1,0:T(8,128)}, f32[384,1024]{1,0:T(8,128)S(1)}, u32[]{:S(2)}) copy-start(f32[384,1024]{1,0:T(8,128)S(1)} %get-tuple-element.87) | copy-start | bytes 4718596
  195.9 10.1 %slice-start = ((s8[8388608]{0:T(1024)(128)(4,1)}), s8[4194304]{0:T(1024)(128)(4,1)S(1)}, s32[]{:S(2)}) async-start(s8[8388608]{0:T(1024)(128)(4,1)} %bitcast.154), calls=%async_computation.11 | async-start | bytes 8388608
  196.3 9.8 %copy-start.13 = (bf16[1,384,1024]{2,1,0:T(8,128)(2,1)S(1)}, bf16[1,384,1024]{2,1,0:T(8,128)(2,1)}, u32[]{:S(2)}) copy-start(bf16[1,384,1024]{2,1,0:T(8,128)(2,1)} %param.27) | copy-start | bytes 2359300
  196.3 9.8 %slice-start.1 = ((s8[8388608]{0:T(1024)(128)(4,1)}), s8[4194304]{0:T(1024)(128)(4,1)S(1)}, s32[]{:S(2)}) async-start(s8[8388608]{0:T(1024)(128)(4,1)} %bitcast.154), calls=%async_computation.12 | async-start | bytes 8388608
  196.3 20.0 %slice-start.2 = ((s8[8388608]{0:T(1024)(128)(4,1)}), s8[4194304]{0:T(1024)(128)(4,1)S(1)}, s32[]{:S(2)}) async-start(s8[8388608]{0:T(1024)(128)(4,1)} %bitcast.156), calls=%async_computation.13 | async-start | bytes 8388608
  206.1 10.2 %slice-start.3 = ((s8[8388608]{0:T(1024)(128)(4,1)}), s8[4194304]{0:T(1024)(128)(4,1)S(1)}, s32[]{:S(2)}) async-start(s8[8388608]{0:T(1024)(128)(4,1)} %bitcast.156), calls=%async_computation.14 | async-start | bytes 8388608
  216.2 3.9 copy-start.29
  279.8 32.5 %copy-start.21 = (f32[1024]{0:T(1024)S(1)}, f32[1024]{0:T(1024)}, u32[]{:S(2)}) copy-start(f32[1024]{0:T(1024)} %get-tuple-element.77) | copy-start | bytes 12292
  318.2 112.2 %reduce-scatter.7.cloned.1.call-start = ((), (), s32[]{:S(2)}) async-start(), calls=%async_computation.7 | async-start | bytes 2359296 | tf_op jit(solution)/shard_map/reduce_scatter | solution.py:647
  320.9 200.2 %reduce-scatter.9.cloned.1.call-start = ((), (), s32[]{:S(2)}) async-start(), calls=%async_computation.8 | async-start | bytes 9437184 | tf_op jit(solution)/shard_map/reduce_scatter | solution.py:646
  331.4 279.8 %reduce-scatter.11.cloned.1.call-start = ((), (), s32[]{:S(2)}) async-start(), calls=%async_computation.9 | async-start | bytes 9437184 | tf_op jit(solution)/shard_map/reduce_scatter | solution.py:645
  343.1 358.9 %all-reduce.6.cloned.1.call-start = ((), (), s32[]{:S(2)}) async-start(), calls=%async_computation.10 | async-start | bytes 6291456 | tf_op jit(solution)/shard_map/psum | solution.py:677
  394.9 216.4 %copy-start.18 = (f32[1024]{0:T(1024)S(1)}, f32[1024]{0:T(1024)}, u32[]{:S(2)}) copy-start(f32[1024]{0:T(1024)} %get-tuple-element.75) | copy-start | bytes 12292
  702.0 2.7 copy-start.15
  702.0 3.5 copy-start.12
  (7 other events, 11.2 us)
Sparse Core Ops, SparseCore 0:
  318.3 74.9 reduce-scatter.4
  396.3 34.1 reduce-scatter.6
  432.7 88.2 reduce-scatter.8
  523.2 87.9 reduce-scatter.10
  615.0 86.8 all-reduce.5

commit v3 on v2

--- a/solution.py
+++ b/solution.py
@@ -336,18 +336,18 @@
 
 def attend_unit(pair, odd, tile, heads_ref, qf_ref, kf_ref, keys_sc, values_t, out_ref, lse_ref):
     length = heads_ref.shape[0]
-    third = heads_ref.shape[1] // 3
     scale = jnp.asarray(1.0 / math.sqrt(DH), BF16)
     cols = pl.ds(pair * LANES, LANES)
+    q_cols, k_cols, v_cols = (pl.ds((3 * pair + i) * LANES, LANES) for i in range(3))
     if not odd:
-        values_t[...] = heads_ref[:, pl.ds(2 * third + pair * LANES, LANES)].T
+        values_t[...] = heads_ref[:, v_cols].T
     mine = own_lanes(odd, (length, LANES))
-    keys_sc[...] = jnp.where(mine, heads_ref[:, pl.ds(third + pair * LANES, LANES)], kf_ref[...])
+    keys_sc[...] = jnp.where(mine, heads_ref[:, k_cols], kf_ref[...])
 
     def one_tile(index, carry):
         rows = aligned(index * tile, tile)
         lanes = own_lanes(odd, (tile, LANES))
-        queries = jnp.where(lanes, heads_ref[rows, cols] * scale, qf_ref[2 * pair + odd, rows, :])
+        queries = jnp.where(lanes, heads_ref[rows, q_cols] * scale, qf_ref[2 * pair + odd, rows, :])
         scores = dot_nt(keys_sc[...], queries)
         top = jnp.max(scores, axis=0, keepdims=True)
         prob = jnp.exp(scores - top)
@@ -508,67 +508,515 @@
     )(qkv_rows, query_feats, key_feats, w_out, w_down, w_in)
 
 
-def attend_backward(
-    tile, q_ref, k_ref, v_ref, qf_ref, kf_ref, go_ref, lse_ref, dq_ref, dk_ref, dv_ref, p_sc, s_sc
+def by_rows(count, body):
+    lax.fori_loop(0, count // 16, lambda i, carry: (body(aligned(i * 16, 16)), carry)[1], 0)
+
+
+class Reduce:
+    def __init__(self, place, grad, out, bufs, sems):
+        self.place, self.grad, self.out = place, grad, out
+        self.rows, self.cols = out.shape
+        self.wide = self.cols // 4
+        self.acc, self.own, self.relay_in, self.quarter_in, self.z_in, self.total = bufs
+        self.own_sem, self.cs, self.rs, self.qs, self.zs, self.fs, self.gs = sems
+
+    @staticmethod
+    def scratch(depth, rows, cols):
+        pair = [pltpu.SemaphoreType.DMA((depth,))] * 2
+        single = [pltpu.SemaphoreType.DMA((2,))] * 2
+        return [
+            pltpu.VMEM((depth, rows, cols), BF16),
+            pltpu.VMEM((rows, cols), BF16),
+            pltpu.VMEM((2, depth, rows, cols // 8), BF16),
+            pltpu.VMEM((2, depth, rows, cols // 4), BF16),
+            pltpu.VMEM((depth, rows, cols // 4), BF16),
+            pltpu.VMEM((rows, cols), BF16),
+            pltpu.SemaphoreType.DMA,
+        ] + pair * 6 + single * 2
+
+    @staticmethod
+    def take(place, grad, out, refs):
+        s = refs[7:]
+        pairs = [(s[i], s[i + 1]) for i in range(0, 16, 2)]
+        sems = (refs[6], pairs[0], pairs[1:3], pairs[3:5], pairs[5], pairs[6], pairs[7])
+        return Reduce(place, grad, out, refs[:6], sems)
+
+    def quarter(self, seat):
+        return aligned(seat * self.wide, self.wide)
+
+    def piece(self, seat, half):
+        return aligned(seat * self.wide + half * (self.wide // 2), self.wide // 2)
+
+    def own_copy(self, step):
+        p = self.place
+        rows = aligned((2 * p.far(step) + p.c) * self.rows, self.rows)
+        return pltpu.make_async_copy(self.grad.at[rows], self.own, self.own_sem)
+
+    def core_copy(self, step):
+        p = self.place
+        rows = aligned((2 * p.far(step) + 1 - p.c) * self.rows, self.rows)
+        return send(self.grad.at[rows], self.acc.at[step], self.cs, step, p.beside)
+
+    def relay_copy(self, step, way):
+        p = self.place
+        src = self.acc.at[step, :, self.piece(p.s3, way)]
+        return send(src, self.relay_in.at[way, step], self.rs[way], step, p.across(way))
+
+    def quarter_copy(self, step, way):
+        p = self.place
+        src = self.acc.at[step, :, self.quarter((p.s1, p.s2)[way])]
+        return send(src, self.quarter_in.at[way, step], self.qs[way], step, p.across(way))
+
+    def z_copy(self, step):
+        p = self.place
+        src = self.acc.at[step, :, self.quarter(p.s)]
+        return send(src, self.z_in.at[step], self.zs, step, p.along(p.far(step)))
+
+    def total_copy(self, way):
+        p = self.place
+        there = self.total.at[:, self.quarter(p.s)]
+        return send(there, there, self.fs, way, p.across(way))
+
+    def total_arrival(self, way):
+        p = self.place
+        there = self.total.at[:, self.quarter((p.s1, p.s2)[way])]
+        return send(there, there, self.fs, way, p.across(way))
+
+    def back_copy(self, way):
+        p = self.place
+        there = self.total.at[:, self.piece((p.s2, p.s1)[way], 1 - way)]
+        return send(there, there, self.gs, way, p.across(way))
+
+    def back_arrival(self, way):
+        p = self.place
+        there = self.total.at[:, self.piece(p.s3, 1 - way)]
+        return send(there, there, self.gs, way, p.across(way))
+
+    def begin(self):
+        depth = self.place.depth
+        self.place.each(1, depth, lambda step: self.core_copy(step).start())
+        self.core_copy(0).start()
+        self.own_copy(1).start()
+
+    def fold(self, step, following):
+        self.core_copy(step).wait_recv()
+        self.own_copy(step).wait()
+        acc, own = self.acc, self.own
+
+        def body(rows):
+            acc[step, rows, :] = (acc[step, rows, :].astype(F32) + own[rows, :].astype(F32)).astype(BF16)
+
+        by_rows(self.rows, body)
+        if following is not None:
+            self.own_copy(following).start()
+        for way in (0, 1):
+            self.relay_copy(step, way).start()
+
+    def swap(self, step):
+        p, acc, half = self.place, self.acc, self.wide // 2
+        for way in (0, 1):
+            self.relay_copy(step, way).wait_recv()
+            cols = self.piece((p.s2, p.s1)[way], way)
+            came = self.relay_in.at[way, step]
+
+            def body(rows):
+                acc[step, rows, cols] = (acc[step, rows, cols].astype(F32) + came[rows, :].astype(F32)).astype(BF16)
+
+            by_rows(self.rows, body)
+        for way in (0, 1):
+            self.quarter_copy(step, way).start()
+
+    def close(self, step, own):
+        p, acc, came = self.place, self.acc, self.quarter_in
+        for way in (0, 1):
+            self.quarter_copy(step, way).wait_recv()
+        cols = self.quarter(p.s)
+
+        def body(rows):
+            acc[step, rows, cols] = (
+                acc[step, rows, cols].astype(F32)
+                + came[0, step, rows, :].astype(F32)
+                + came[1, step, rows, :].astype(F32)
+            ).astype(BF16)
+
+        by_rows(self.rows, body)
+        if not own:
+            self.z_copy(step).start()
+
+    def collect(self):
+        p, acc, came, total = self.place, self.acc, self.z_in, self.total
+        p.each(1, p.depth, lambda step: self.z_copy(step).wait_recv())
+        cols = self.quarter(p.s)
+
+        def body(rows):
+            start = acc[0, rows, cols].astype(F32)
+            if p.depth <= 8:
+                for step in range(1, p.depth):
+                    start = start + came[step, rows, :].astype(F32)
+            else:
+                start = lax.fori_loop(1, p.depth, lambda step, sofar: sofar + came[step, rows, :].astype(F32), start)
+            total[rows, cols] = start.astype(BF16)
+
+        by_rows(self.rows, body)
+        for way in (0, 1):
+            self.total_copy(way).start()
+
+    def spread(self):
+        for way in (0, 1):
+            self.total_arrival(way).wait_recv()
+        for way in (0, 1):
+            self.back_copy(way).start()
+
+    def finish(self):
+        for way in (0, 1):
+            self.back_arrival(way).wait_recv()
+        total, out = self.total, self.out
+
+        def body(rows):
+            out[rows, :] = total[rows, :].astype(F32)
+
+        by_rows(self.rows, body)
+
+        def done(step):
+            self.core_copy(step).wait_send()
+            for way in (0, 1):
+                self.relay_copy(step, way).wait_send()
+                self.quarter_copy(step, way).wait_send()
+
+        self.place.each(0, self.place.depth, done)
+        self.place.each(1, self.place.depth, lambda step: self.z_copy(step).wait_send())
+        for way in (0, 1):
+            self.total_copy(way).wait_send()
+            self.back_copy(way).wait_send()
+
+
+REDUCE_REFS = 23
+
+
+def reduce_steps(place, reduces, between):
+    depth = place.depth
+    work = list(between)
+
+    def gap():
+        if work:
+            work.pop(0)()
+
+    if depth <= 8:
+        order = [(t + 1) % depth for t in range(depth)]
+        for t in range(depth + 2):
+            for one in reduces:
+                if t < depth:
+                    one.fold(order[t], order[t + 1] if t + 1 < depth else None)
+            for one in reduces:
+                if 0 <= t - 1 < depth:
+                    one.swap(order[t - 1])
+            for one in reduces:
+                if 0 <= t - 2 < depth:
+                    one.close(order[t - 2], order[t - 2] == 0)
+            gap()
+    else:
+        def run(first, last, body):
+            lax.fori_loop(first, last, lambda step, carry: (body(step), carry)[1], 0)
+
+        for one in reduces:
+            run(1, depth, lambda step: one.fold(step, lax.rem(step + 1, depth)))
+            one.fold(0, None)
+            run(0, depth, one.swap)
+            run(1, depth, lambda step: one.close(step, False))
+            one.close(0, True)
+    for one in reduces:
+        one.collect()
+    gap()
+    for one in reduces:
+        one.spread()
+    gap()
+    for rest in work:
+        rest()
+
+
+def backward_unit(
+    pair, odd, half, tile, heads_ref, qf_ref, kf_ref, go_ref, lse_ref, out_ref, keys_sc, values_sc, keys_t, p_sc, s_sc, k_acc, v_acc
 ):
-    length = k_ref.shape[0]
+    length = heads_ref.shape[0]
+    span = p_sc.shape[1]
     scale = jnp.asarray(1.0 / math.sqrt(DH), BF16)
-    keys_t = k_ref[...].T
-    for odd in (0, 1):
-        mine = own_lanes(odd, (length, LANES))
-        keys = jnp.where(mine, k_ref[...], kf_ref[...])
-        values = jnp.where(mine, v_ref[...], jnp.zeros((), BF16))
-        for start in range(0, length, tile):
-            rows = pl.ds(start, tile)
-            lanes = own_lanes(odd, (tile, LANES))
-            queries = jnp.where(lanes, q_ref[rows, :] * scale, qf_ref[odd, rows, :])
-            prob = jnp.exp(dot_nt(keys, queries) - lse_ref[0, odd, rows][None, :])
-            grad_prob = dot_nt(values, go_ref[rows, :])
-            delta = jnp.sum(prob * grad_prob, axis=0, keepdims=True)
-            p_sc[:, rows] = prob.astype(BF16)
-            s_sc[:, rows] = (prob * (grad_prob - delta)).astype(BF16)
-        grad_v = dot_nn(p_sc[...], go_ref[...]).astype(BF16)
-        grad_k = dot_nn(s_sc[...], q_ref[...] * scale).astype(BF16)
-        grad_q = (dot_nn(keys_t, s_sc[...]) * (1.0 / math.sqrt(DH))).T.astype(BF16)
+    q_cols, k_cols, v_cols = (pl.ds((3 * pair + i) * LANES, LANES) for i in range(3))
+    cols = pl.ds(pair * LANES, LANES)
+    mine = own_lanes(odd, (length, LANES))
+    if half == 0:
+        keys_sc[...] = jnp.where(mine, heads_ref[:, k_cols], kf_ref[...])
+        values_sc[...] = jnp.where(mine, heads_ref[:, v_cols], jnp.zeros((), BF16))
+        if not odd:
+            keys_t[...] = heads_ref[:, k_cols].T
+
+    def one_tile(index, carry):
+        here = aligned(index * tile, tile)
+        rows = aligned(half * span + index * tile, tile)
+        lanes = own_lanes(odd, (tile, LANES))
+        queries = jnp.where(lanes, heads_ref[rows, q_cols] * scale, qf_ref[2 * pair + odd, rows, :])
+        prob = jnp.exp(dot_nt(keys_sc[...], queries) - lse_ref[pair, pl.ds(odd, 1), rows])
+        grad_prob = dot_nt(values_sc[...], go_ref[rows, cols])
+        delta = jnp.sum(prob * grad_prob, axis=0, keepdims=True)
+        p_sc[:, here] = prob.astype(BF16)
+        s_sc[:, here] = (prob * (grad_prob - delta)).astype(BF16)
+        return carry
+
+    lax.fori_loop(0, span // tile, one_tile, 0)
+    part = pl.ds(half * span, span)
+    grad_v = dot_nn(p_sc[...], go_ref[part, cols])
+    grad_k = dot_nn(s_sc[...], heads_ref[part, q_cols] * scale)
+    grad_q = (dot_nn(keys_t[...], s_sc[...]) * (1.0 / math.sqrt(DH))).T.astype(BF16)
+    last = half * span + span == length
+
+    def put(rows, columns, value, keep):
         if odd:
-            dv_ref[...] = jnp.where(mine, grad_v, dv_ref[...])
-            dk_ref[...] = jnp.where(mine, grad_k, dk_ref[...])
-            dq_ref[...] = jnp.where(mine, grad_q, dq_ref[...])
-        else:
-            dv_ref[...] = grad_v
-            dk_ref[...] = grad_k
-            dq_ref[...] = grad_q
-
-
-def column_spec(length, offset):
-    return pl.BlockSpec((length, LANES), lambda p: (0, p + offset))
-
-
-def attention_backward(by_heads, query_feats, key_feats, grad_out, lse):
+            value = jnp.where(keep, value, out_ref[rows, columns])
+        out_ref[rows, columns] = value
+
+    put(part, q_cols, grad_q, own_lanes(odd, (span, LANES)))
+    if half > 0:
+        grad_v, grad_k = grad_v + v_acc[...], grad_k + k_acc[...]
+    if last:
+        put(pl.ds(0, length), k_cols, grad_k.astype(BF16), mine)
+        put(pl.ds(0, length), v_cols, grad_v.astype(BF16), mine)
+    else:
+        v_acc[...], k_acc[...] = grad_v, grad_k
+
+
+def backward_kernel(
+    fsdp_count,
+    go_rows_ref,
+    heads_ref,
+    qf_ref,
+    kf_ref,
+    lse_ref,
+    out_g_ref,
+    down_g_ref,
+    in_g_ref,
+    dqkv_all,
+    out_total,
+    down_total,
+    in_total,
+    go_sc,
+    grads_sc,
+    keys_sc,
+    values_sc,
+    keys_t,
+    p_sc,
+    s_sc,
+    k_acc,
+    v_acc,
+    *rest,
+):
+    place = Place(fsdp_count)
+    rows = go_rows_ref.shape[0]
+    reduces = [
+        Reduce.take(place, grad, out, rest[i * REDUCE_REFS : (i + 1) * REDUCE_REFS])
+        for i, (grad, out) in enumerate(
+            ((out_g_ref, out_total), (in_g_ref, in_total), (down_g_ref, down_total))
+        )
+    ]
+    g_own, g_sent, g_got, d_sent, d_got, d_own = rest[3 * REDUCE_REFS :]
+    seats = (place.s1, place.s2, place.s3)
+    width = go_sc.shape[1]
+    pairs = width // LANES
+    block = 3 * LANES
+
+    def part(seat):
+        return go_rows_ref.at[:, aligned(seat * width, width)]
+
+    def slot(seat):
+        return go_sc.at[aligned(seat * rows, rows)]
+
+    def grad_copy(pair, way):
+        src = grads_sc.at[aligned(seats[way] * rows, rows), pl.ds(pair * block, block)]
+        dst = dqkv_all.at[:, aligned((place.s * pairs + pair) * block, block)]
+        return send(src, dst, (d_sent, d_got), pair * 3 + way, place.across(way))
+
+    def grad_own(pair):
+        src = grads_sc.at[aligned(place.s * rows, rows), pl.ds(pair * block, block)]
+        dst = dqkv_all.at[:, aligned((place.s * pairs + pair) * block, block)]
+        return pltpu.make_async_copy(src, dst, d_own.at[pair])
+
+    def grad_arrival(pair, way):
+        there = dqkv_all.at[:, aligned((seats[way] * pairs + pair) * block, block)]
+        return send(there, there, (d_sent, d_got), pair * 3 + way, place.across(way))
+
+    place.meet()
+    for way in range(3):
+        send(part(seats[way]), slot(place.s), (g_sent, g_got), way, place.across(way)).start()
+    own = pltpu.make_async_copy(part(place.s), slot(place.s), g_own)
+    own.start()
+    for one in reduces:
+        one.begin()
+    own.wait()
+    for way in range(3):
+        send(slot(seats[way]), slot(seats[way]), (g_sent, g_got), way, place.across(way)).wait_recv()
+
+    def unit(pair, odd, half):
+        backward_unit(
+            pair, odd, half, 256, heads_ref, qf_ref, kf_ref, go_sc, lse_ref, grads_sc,
+            keys_sc, values_sc, keys_t, p_sc, s_sc, k_acc, v_acc,
+        )
+        if odd and half:
+            for way in range(3):
+                grad_copy(pair, way).start()
+            grad_own(pair).start()
+
+    reduce_steps(
+        place,
+        reduces,
+        [functools.partial(unit, pair, odd, half) for pair in range(pairs) for odd in (0, 1) for half in (0, 1)],
+    )
+    for way in range(3):
+        send(part(seats[way]), slot(place.s), (g_sent, g_got), way, place.across(way)).wait_send()
+        for pair in range(pairs):
+            grad_copy(pair, way).wait_send()
+            grad_arrival(pair, way).wait_recv()
+    for pair in range(pairs):
+        grad_own(pair).wait()
+    for one in reduces:
+        one.finish()
+
+
+def backward_attention(fsdp_count, grad_att, by_heads, query_feats, key_feats, lse, grad_out, grad_down, grad_in):
+    rows, width = grad_att.shape
     length = by_heads.shape[0]
-    heads = query_feats.shape[0]
-    pairs = heads // 2
-    shape = jax.ShapeDtypeStruct((length, heads * DH), BF16)
+    own_width = width // 4
+    depth = fsdp_count // 2
+    span = length // 2
+    anywhere = pl.BlockSpec(memory_space=pl.ANY)
+    vmem = pl.BlockSpec(memory_space=pltpu.VMEM)
+    grads = (grad_out, grad_in, grad_down)
+
+    def kept(grad):
+        return jax.ShapeDtypeStruct((grad.shape[0] // fsdp_count, grad.shape[1]), F32)
+
+    reduce_scratch = []
+    for grad in grads:
+        reduce_scratch += Reduce.scratch(depth, *kept(grad).shape)
     return pl.pallas_call(
-        functools.partial(attend_backward, 256),
-        grid=(pairs,),
-        out_shape=(shape, shape, shape),
-        in_specs=[
-            column_spec(length, 0),
-            column_spec(length, pairs),
-            column_spec(length, 2 * pairs),
-            pl.BlockSpec((2, length, LANES), lambda p: (p, 0, 0)),
-            pl.BlockSpec((length, LANES), lambda p: (0, 0)),
-            column_spec(length, 0),
-            pl.BlockSpec((1, 2, length), lambda p: (p, 0, 0)),
+        functools.partial(backward_kernel, fsdp_count),
+        out_shape=(
+            jax.ShapeDtypeStruct((rows, 3 * width), BF16),
+            kept(grad_out),
+            kept(grad_down),
+            kept(grad_in),
+        ),
+        in_specs=[anywhere, vmem, vmem, vmem, vmem, anywhere, anywhere, anywhere],
+        out_specs=(anywhere, vmem, vmem, vmem),
+        scratch_shapes=[
+            pltpu.VMEM((length, own_width), BF16),
+            pltpu.VMEM((length, 3 * own_width), BF16),
+            pltpu.VMEM((length, LANES), BF16),
+            pltpu.VMEM((length, LANES), BF16),
+            pltpu.VMEM((LANES, length), BF16),
+            pltpu.VMEM((length, span), BF16),
+            pltpu.VMEM((length, span), BF16),
+            pltpu.VMEM((length, LANES), F32),
+            pltpu.VMEM((length, LANES), F32),
+        ]
+        + reduce_scratch
+        + [
+            pltpu.SemaphoreType.DMA,
+            pltpu.SemaphoreType.DMA((3,)),
+            pltpu.SemaphoreType.DMA((3,)),
+            pltpu.SemaphoreType.DMA((3 * own_width // LANES,)),
+            pltpu.SemaphoreType.DMA((3 * own_width // LANES,)),
+            pltpu.SemaphoreType.DMA((own_width // LANES,)),
         ],
-        out_specs=(column_spec(length, 0), column_spec(length, 0), column_spec(length, 0)),
-        scratch_shapes=[pltpu.VMEM((length, length), BF16), pltpu.VMEM((length, length), BF16)],
-        compiler_params=pltpu.CompilerParams(vmem_limit_bytes=56 << 20),
-        cost_estimate=pl.CostEstimate(
-            flops=heads * length * length * 1280, bytes_accessed=12 << 20, transcendentals=heads * length * length
+        compiler_params=pltpu.CompilerParams(
+            collective_id=3, has_side_effects=True, vmem_limit_bytes=60 << 20
         ),
-    )(by_heads, by_heads, by_heads, query_feats, key_feats, grad_out, lse)
+    )(grad_att, by_heads, query_feats, key_feats, lse, grad_out, grad_down, grad_in)
+
+
+def last_reduce_kernel(fsdp_count, grad_ref, small_ref, total_ref, small_total, mine_in, z_in, x_in, own_sc, *rest):
+    place = Place(fsdp_count)
+    big = Reduce.take(place, grad_ref, total_ref, rest[:REDUCE_REFS])
+    c_sent, c_got, z_sent, z_got, x_sent, x_got = rest[REDUCE_REFS:]
+    size = small_total.shape[0]
+    depth = place.depth
+
+    def rows_of(z, core):
+        return aligned((2 * z + core) * size, size)
+
+    def core_copy(step):
+        src = small_ref.at[rows_of(place.far(step), 1 - place.c)]
+        return send(src, mine_in.at[step], (c_sent, c_got), step, place.beside)
+
+    def z_copy(step):
+        return send(own_sc.at[step], z_in.at[step], (z_sent, z_got), step, place.along(place.far(step)))
+
+    def x_copy(way):
+        return send(own_sc.at[0], x_in.at[way], (x_sent, x_got), way, place.across(way))
+
+    def fold(step):
+        core_copy(step).wait_recv()
+        own_sc[step] = small_ref[rows_of(place.far(step), place.c), :] + mine_in[step]
+
+    def along(step):
+        fold(step)
+        z_copy(step).start()
+
+    def gather_z(step):
+        z_copy(step).wait_recv()
+        own_sc[0] = own_sc[0] + z_in[step]
+
+    place.meet()
+    place.each(0, depth, lambda step: core_copy(step).start())
+    big.begin()
+    fold(0)
+    place.each(1, depth, along)
+
+    def small_middle():
+        place.each(1, depth, gather_z)
+        for way in range(3):
+            x_copy(way).start()
+
+    def small_end():
+        for way in range(3):
+            x_copy(way).wait_recv()
+        small_total[...] = own_sc[0] + x_in[0] + x_in[1] + x_in[2]
+
+    reduce_steps(place, [big], [small_middle, small_end])
+    place.each(0, depth, lambda step: core_copy(step).wait_send())
+    place.each(1, depth, lambda step: z_copy(step).wait_send())
+    for way in range(3):
+        x_copy(way).wait_send()
+    big.finish()
+
+
+def last_reduce(fsdp_count, grad, small):
+    anywhere = pl.BlockSpec(memory_space=pl.ANY)
+    vmem = pl.BlockSpec(memory_space=pltpu.VMEM)
+    depth = fsdp_count // 2
+    size = small.shape[0] // fsdp_count
+    kept = (grad.shape[0] // fsdp_count, grad.shape[1])
+    return pl.pallas_call(
+        functools.partial(last_reduce_kernel, fsdp_count),
+        out_shape=(jax.ShapeDtypeStruct(kept, F32), jax.ShapeDtypeStruct((size, LANES), F32)),
+        in_specs=[anywhere, vmem],
+        out_specs=(vmem, vmem),
+        scratch_shapes=[
+            pltpu.VMEM((depth, size, LANES), F32),
+            pltpu.VMEM((depth, size, LANES), F32),
+            pltpu.VMEM((3, size, LANES), F32),
+            pltpu.VMEM((depth, size, LANES), F32),
+        ]
+        + Reduce.scratch(depth, *kept)
+        + [
+            pltpu.SemaphoreType.DMA((depth,)),
+            pltpu.SemaphoreType.DMA((depth,)),
+            pltpu.SemaphoreType.DMA((depth,)),
+            pltpu.SemaphoreType.DMA((depth,)),
+            pltpu.SemaphoreType.DMA((3,)),
+            pltpu.SemaphoreType.DMA((3,)),
+        ],
+        compiler_params=pltpu.CompilerParams(
+            collective_id=4, has_side_effects=True, vmem_limit_bytes=48 << 20
+        ),
+    )(grad, small)
 
 
 def swap_thirds(rows, outer, inner):
@@ -594,7 +1042,7 @@
     b_down,
     cotangent,
 ):
-    width = w_qkv.shape[1] // 3
+    groups = w_qkv.shape[1] // (3 * LANES)
     share = ln1_gain.shape[0]
     packed = jnp.concatenate([ln1_gain, ln1_bias, ln2_gain, ln2_bias, b_down, b_in])
     packed_rows = -(-packed.shape[0] // (16 * LANES)) * 16
@@ -602,7 +1050,7 @@
     tok_count = segment_ids.shape[1]
     seg_rows = -(-tok_count // (8 * LANES)) * 8
     seg = jnp.pad(segment_ids[0], (0, seg_rows * LANES - tok_count)).reshape(seg_rows, LANES)
-    qkv_weight, packed, seg = first_gather(fsdp_count, swap_thirds(w_qkv, 3, seq_count), packed, seg)
+    qkv_weight, packed, seg = first_gather(fsdp_count, swap_thirds(w_qkv, 3, groups), packed, seg)
     packed = packed.reshape(fsdp_count, packed_rows * LANES).astype(F32)
     gain_one, bias_one, gain_two, bias_two, down_bias = (
         packed[:, i * share : (i + 1) * share].reshape(-1) for i in range(5)
@@ -638,18 +1086,18 @@
     )
     hidden_low = grad_hidden.astype(BF16)
     grad_att = dot_nt(hidden_low, out_weight).astype(BF16)
-    grad_att_heads = lax.all_to_all(grad_att, "seq", split_axis=1, concat_axis=0, tiled=True)
-    scatter = functools.partial(
-        lax.psum_scatter, axis_name="fsdp", scatter_dimension=0, tiled=True
+    grad_qkv_rows, total_out, total_down, total_in = backward_attention(
+        fsdp_count,
+        grad_att,
+        by_heads,
+        query_feats,
+        key_feats,
+        lse,
+        dot_tn(att_rows, hidden_low).astype(BF16),
+        dot_tn(act_low, cot_low).astype(BF16),
+        dot_tn(normed_two, grad_pre).astype(BF16),
     )
-    share_down = scatter(dot_tn(act_low, cot_low).astype(BF16))
-    share_in = scatter(dot_tn(normed_two, grad_pre).astype(BF16))
-    share_out = scatter(dot_tn(att_rows, hidden_low).astype(BF16))
-    grad_heads = jnp.concatenate(
-        attention_backward(by_heads, query_feats, key_feats, grad_att_heads, lse), axis=1
-    )
-    grad_qkv_rows = lax.all_to_all(grad_heads, "seq", split_axis=0, concat_axis=1, tiled=True)
-    share_qkv = scatter(dot_tn(normed_one, grad_qkv_rows).astype(BF16))
+    grad_qkv = dot_tn(normed_one, grad_qkv_rows).astype(BF16)
     grad_norm_one = dot_nt(grad_qkv_rows, qkv_weight)
     scaled_one = grad_norm_one * gain_one
     grad_tokens = (
@@ -671,24 +1119,23 @@
         jnp.sum(grad_pre.astype(F32), axis=0),
     ]
     small = jnp.concatenate([v.reshape(fsdp_count, -1) for v in small], axis=1)
-    small = lax.psum(small, ("seq", "fsdp"))
-    small = lax.dynamic_index_in_dim(small, lax.axis_index("fsdp"), 0, keepdims=False)
-    parts = [small[i * share : (i + 1) * share] for i in range(5)] + [small[5 * share :]]
-    total_down, total_in, total_out, total_qkv = lax.psum(
-        (share_down, share_in, share_out, share_qkv), "seq"
-    )
+    small = jnp.pad(small, ((0, 0), (0, packed_rows * LANES - small.shape[1])))
+    total_qkv, small = last_reduce(fsdp_count, grad_qkv, small.reshape(-1, LANES))
+    small = small.reshape(-1)
+    parts = [small[i * share : (i + 1) * share] for i in range(5)]
+    parts.append(small[5 * share : 5 * share + b_in.shape[0]])
     return (
         result.astype(BF16)[None],
         grad_tokens[None],
         parts[0],
         parts[1],
-        swap_thirds(total_qkv, seq_count, 3).astype(F32),
-        total_out.astype(F32),
+        swap_thirds(total_qkv, groups, 3),
+        total_out,
         parts[2],
         parts[3],
-        total_in.astype(F32),
+        total_in,
         parts[5],
-        total_down.astype(F32),
+        total_down,
         parts[4],
     )
 

time: 725 us -> 474 us (0.65)
  waiting for transfers between devices: 295 us -> 0 us
  Pallas kernels: 182 us -> 354 us
  blocking collectives: 91.9 us -> 0 us
  matrix products: 79.5 us -> 65.6 us
  between operations: 14.8 us -> 1.7 us
    reduce_scatter x4 -> x0, waiting for transfers between devices: 265 us -> none  [the longest x1 90.6 us: per_device(): share_in = scatter(dot_tn(normed_two, grad_pre).astype(BF16))]
    pallas_call x1 -> x2, Pallas kernels: 27.9 us -> 200 us  [the longest x1 154 us: backward_attention(): pl.pallas_call(functools.partial(backward_kernel, fsdp_count), out_shape=...]
    all_to_all x2 -> x0, blocking collectives: 53.5 us -> none  [the longest x1 31.1 us: per_device(): lax.all_to_all(grad_heads, 'seq', split_axis=0, concat_axis=1, tiled=True)]
    psum x1 -> x0, blocking collectives: 38.4 us -> none  [per_device(): small = lax.psum(small, ('seq', 'fsdp'))]
    psum x1 -> x0, waiting for transfers between devices: 30 us -> none  [per_device(): lax.psum((share_down, share_in, share_out, share_qkv), 'seq')]
    dot_general x4, matrix products: 27.3 us -> 19.1 us  [dot_nn(): return jnp.dot(a, b, preferred_element_type=F32)]
  transfers between devices with their start and end apart: 5 -> 0, of which waited for: 5 -> 0; matrix products, arithmetic and copies ran while one was open for 7% -> 0% of each run, Pallas kernels for 0% -> 0%
where the time goes in v3:
time: 474 us; the launch traced here: 465 us
  Pallas kernels  354 us (75%)
  matrix products  65.6 us (14%)
  local copies, waits for them, and re-layouts  34.6 us (7%)
  other arithmetic  8.87 us (2%)
    pallas_call x1, Pallas kernels, backward_attention(): pl.pallas_call(functools.partial(backward_kernel, fsdp_count), out_shape=...  154 us
    pallas_call x1, Pallas kernels, forward_attention(): pl.pallas_call(functools.partial(forward_kernel, fsdp_count), out_shape=(...  109 us
    pallas_call x1, Pallas kernels, last_reduce(): pl.pallas_call(functools.partial(last_reduce_kernel, fsdp_count), out_sha...  46.1 us
    pallas_call x1, Pallas kernels, first_gather(): pl.pallas_call(functools.partial(first_gather_kernel, fsdp_count), out_sh...  45.2 us
    dot_general x4, matrix products, dot_tn(): lax.dot_general(a, b, (((0,), (0,)), ((), ())), preferred_element_type=F32)  24.6 us
    dot_general x4, matrix products, dot_nt(): lax.dot_general(a, b, (((1,), (1,)), ((), ())), preferred_element_type=F32)  22 us
    dot_general x4, matrix products, dot_nn(): return jnp.dot(a, b, preferred_element_type=F32)  19.1 us
    unnamed x78, local copies, waits for them, and re-layouts  14.1 us

profile of v3, /device:TPU:0, one launch (start us, length us, event | category | flops | bytes accessed | tf_op | source)
XLA Modules:
  0.0 464.7 jit_solution(18123357337926931641)
XLA Ops:
  2.0 1.3 convert_reduce_fusion.2
  3.4 1.5 fusion.25
  4.9 0.8 dynamic-update-slice.6
  5.8 0.8 dynamic-update-slice.7
  6.6 0.8 dynamic-update-slice.8
  9.1 0.9 dynamic-update-slice.11
  12.3 1.2 copy.41.w_ref
  13.7 45.2 %shard_map.229 = (bf16[1024,3072]{1,0:T(8,128)(2,1)}, bf16[128,128]{1,0:T(8,128)(2,1)}, s32[32,128]{1,0:T(8,128)}) custom-call(bf16[128,3072]{1,0:T(8,128)(2,1)} %copy.41.w_ref, bf16[16,128]{1,0:T(8,128)(2,1)} %pad_bitcast_fusion.1.vec_ref, s32[8,128]{1,0:T(8,128)} %pad_bitcast_fusion.seg_ref), custom_call_target="tpu_custom_call" | custom-call | tf_op jit(solution)/shard_map/pallas_call | solution.py:322
  62.0 1.1 concatenate.18.kf_ref
  63.1 1.3 broadcast_in_dim.61
  64.5 1.3 broadcast_in_dim.62
  65.8 9.4 %concatenate.17.qf_ref = bf16[4,1536,128]{2,1,0:T(8,128)(2,1)S(1)} concatenate(bf16[4,1536,24]{2,1,0:T(8,128)(2,1)S(1)} %bitcast.128, bf16[4,1536,6]{2,1,0:T(8,128)(2,1)} %broadcast_in_dim.61, bf16[4,1536,34]{2,1,0:T(8,128)(2,1)} %broadcast_in_dim.62, bf16[4,1536,24]{2,1,0:T(8,128)(2,1)S(1)} %bitcast.129, bf16[4,1536,6]{2,1,0:T(8,128)(2,1)} %broadcast_in_dim.61, ...), dimensions={2} | concatenate | bytes 3145728 | tf_op jit(solution)/shard_map/concatenate | solution.py:75
  75.2 6.3 %convolution_convert_fusion.3.qkv_ref = bf16[384,3072]{1,0:T(8,128)(2,1)S(1)} fusion(bf16[1024,3072]{1,0:T(8,128)(2,1)} %get-tuple-element.28, bf16[1,384,1024]{2,1,0:T(8,128)(2,1)} %param.14, f32[1024]{0:T(1024)} %get-tuple-element.79, f32[1024]{0:T(1024)S(1)} %get-tuple-element.80, f32[384]{0:T(512)S(1)} %add_rsqrt_fusion.1, ...), kind=kOutput, calls=%fused_computation.21 | convolution fusion | flops 2419458048 | bytes 9448448 | tf_op jit(solution)/shard_map/dot_general | solution.py:35
  81.7 108.8 %shard_map.230 = (bf16[1536,768]{1,0:T(8,128)(2,1)S(1)}, f32[2,2,1536]{2,1,0:T(2,128)S(1)}, bf16[384,1024]{1,0:T(8,128)(2,1)S(1)}, bf16[1024,1024]{1,0:T(8,128)(...) custom-call(bf16[384,3072]{1,0:T(8,128)(2,1)S(1)} %convolution_convert_fusion.3.qkv_ref, ...), custom_call_target="tpu_custom_call" | custom-call | tf_op jit(solution)/shard_map/pallas_call | solution.py:477
  190.5 1.1 fusion.41
  192.9 6.8 %convolution_add_fusion = f32[384,4096]{1,0:T(8,128)S(1)} fusion(bf16[1024,4096]{1,0:T(8,128)(2,1)} %get-tuple-element.32, f32[4096]{0:T(1024)S(1)} %bitcast.134, f32[384,1024]{1,0:T(8,128)S(1)} %get-tuple-element.89, f32[1024]{0:T(1024)S(1)} %copy-done.19, f32[1024]{0:T(1024)S(1)} %get-tuple-element.76, f32[384]{0:T(512)S(1)} %add_rsqrt_fusion, ...), kind=kOutput, calls=%fused_computation.20 | convolution fusion | flops 3224764416 | bytes 16280576 | tf_op jit(solution)/shard_map/dot_general | solution.py:35
  199.8 4.9 %fusion.26 = bf16[1,384,1024]{2,1,0:T(8,128)(2,1)} fusion(f32[384,1024]{1,0:T(8,128)S(1)} %get-tuple-element.89, bf16[4096,1024]{1,0:T(8,128)(2,1)S(1)} %bitcast.138, f32[1024]{0:T(1024)S(1)} %copy-done.20, f32[384,4096]{1,0:T(8,128)S(1)} %convolution_add_fusion), kind=kOutput, calls=%fused_computation.53 | convolution fusion | flops 3236560896 | bytes 17043456 | tf_op jit(solution)/shard_map/dot_general | solution.py:35
  204.7 8.9 %convert_reduce_fusion = (f32[4096]{0:T(1024)S(1)}, bf16[384,4096]{1,0:T(8,128)(2,1)S(1)}) fusion(f32[384,4096]{1,0:T(8,128)S(1)} %convolution_add_fusion, bf16[4096,1024]{1,0:T(8,128)(2,1)S(1)} %bitcast.138, bf16[1,384,1024]{2,1,0:T(8,128)(2,1)S(1)} %copy-done.15), kind=kOutput, calls=%fused_computation.17 | convolution fusion | flops 3262115840 | bytes 18628608 | tf_op jit(solution)/shard_map/dot_general | solution.py:39
  213.6 4.9 %multiply_reduce_fusion = (f32[1024]{0:T(1024)S(1)}, f32[384]{0:T(512)S(1)}, f32[384]{0:T(512)S(1)}, f32[1024]{0:T(1024)S(1)}, f32[384,1024]{1,0:T(8,128)}) fusion(f32[384,1024]{1,0:T(8,128)S(1)} %get-tuple-element.89, f32[384]{0:T(512)S(1)} %add_rsqrt_fusion, f32[384]{0:T(512)S(1)} %broadcast_multiply_fusion.4, f32[1024]{0:T(1024)S(1)} %get-tuple-element.76, ...), kind=kOutput, calls=%fused_computation.44 | convolution fusion | flops 3224761344 | bytes 14698496 | tf_op jit(solution)/shard_map/dot_general | solution.py:39
  218.6 2.7 convert_reduce_fusion.1
  221.3 1.9 convolution_convert_fusion.5.go_rows_ref
  223.2 2.6 convolution_convert_fusion.4.out_g_ref
  225.8 7.3 %convolution_convert_fusion.1.down_g_ref = bf16[4096,1024]{1,0:T(8,128)(2,1)} fusion(bf16[1,384,1024]{2,1,0:T(8,128)(2,1)S(1)} %copy-done.15, f32[384,4096]{1,0:T(8,128)S(1)} %bitcast.140), kind=kOutput, calls=%fused_computation.5 | convolution fusion | flops 3239575552 | bytes 15466496 | tf_op jit(solution)/shard_map/dot_general | solution.py:43
  233.2 7.4 %convolution_convert_fusion.in_g_ref = bf16[1024,4096]{1,0:T(8,128)(2,1)} fusion(bf16[384,4096]{1,0:T(8,128)(2,1)S(1)} %copy-done.22, f32[384,1024]{1,0:T(8,128)S(1)} %copy-done.12, f32[1024]{0:T(1024)S(1)} %copy-done.19, f32[1024]{0:T(1024)S(1)} %get-tuple-element.76, f32[384]{0:T(512)S(1)} %add_rsqrt_fusion, f32[384]{0:T(512)S(1)} %broadcast_multiply_fusion.4), kind=kOutput, calls=%fused_computation.4 | convolution fusion | flops 3227385856 | bytes 13118464 | tf_op jit(solution)/shard_map/dot_general | solution.py:43
  240.5 153.7 %shard_map.231 = (bf16[384,3072]{1,0:T(8,128)(2,1)}, f32[128,1024]{1,0:T(8,128)}, f32[512,1024]{1,0:T(8,128)}, f32[128,4096]{1,0:T(8,128)}) custom-call(bf16[384,1024]{1,0:T(8,128)(2,1)} %convolution_convert_fusion.5.go_rows_ref, bf16[1536,768]{1,0:T(8,128)(2,1)} %copy-done.2, bf16[4,1536,128]{2,1,0:T(8,128)(2,1)} %copy-done, bf16[1536,128]{1,0:T(8,128)(2,1)} %copy-done.1, ...), custom_call_target="tpu_custom_call" | custom-call | tf_op jit(solution)/shard_map/pallas_call | solution.py:898
  394.2 6.2 %fusion.24 = (f32[1024]{0:T(1024)S(1)}, f32[384]{0:T(512)S(1)}, f32[384]{0:T(512)S(1)}, f32[1024]{0:T(1024)S(1)}, f32[384,1024]{1,0:T(8,128)S(1)}) fusion(bf16[1,384,1024]{2,1,0:T(8,128)(2,1)S(1)} %copy-done.10, f32[384]{0:T(512)S(1)} %add_rsqrt_fusion.1, f32[384]{0:T(512)S(1)} %broadcast_multiply_fusion.5, f32[1024]{0:T(1024)S(1)} %get-tuple-element.80, ...), kind=kOutput, calls=%fused_computation.42 | convolution fusion | flops 2419848192 | bytes 11028480 | tf_op jit(solution)/shard_map/dot_general | solution.py:39
  400.5 1.5 fusion.27
  402.1 7.3 %convolution_convert_fusion.2.grad_ref = bf16[1024,3072]{1,0:T(8,128)(2,1)} fusion(bf16[384,3072]{1,0:T(8,128)(2,1)} %get-tuple-element.36, bf16[1,384,1024]{2,1,0:T(8,128)(2,1)S(1)} %copy-done.10, f32[1024]{0:T(1024)S(1)} %copy-done.18, f32[1024]{0:T(1024)S(1)} %get-tuple-element.80, f32[384]{0:T(512)S(1)} %add_rsqrt_fusion.1, ...), kind=kOutput, calls=%fused_computation.19 | convolution fusion | flops 2421424128 | bytes 9448448 | tf_op jit(solution)/shard_map/dot_general | solution.py:43
  409.4 46.1 %shard_map.232 = (f32[128,3072]{1,0:T(8,128)S(1)}, f32[16,128]{1,0:T(8,128)S(1)}) custom-call(bf16[1024,3072]{1,0:T(8,128)(2,1)} %convolution_convert_fusion.2.grad_ref, f32[128,128]{1,0:T(8,128)S(1)} %reshape.233.small_ref), custom_call_target="tpu_custom_call" | custom-call | tf_op jit(solution)/shard_map/pallas_call | solution.py:996
  456.2 1.6 copy.46
  459.7 3.3 copy.63
  463.0 1.3 copy.64
  (111 shorter events, 12.7 us)
Async XLA Ops:
  0.6 11.2 %copy-start.14 = (bf16[128,3072]{1,0:T(8,128)(2,1)S(1)}, bf16[128,3072]{1,0:T(8,128)(2,1)}, u32[]{:S(2)}) copy-start(bf16[128,3072]{1,0:T(8,128)(2,1)} %param.19) | copy-start | bytes 2359300
  63.1 18.5 %copy-start.1 = (bf16[1536,128]{1,0:T(8,128)(2,1)}, bf16[1536,128]{1,0:T(8,128)(2,1)S(1)}, u32[]{:S(2)}) copy-start(bf16[1536,128]{1,0:T(8,128)(2,1)S(1)} %concatenate.18.kf_ref) | copy-start | bytes 1179652
  75.2 6.4 %copy-start = (bf16[4,1536,128]{2,1,0:T(8,128)(2,1)}, bf16[4,1536,128]{2,1,0:T(8,128)(2,1)S(1)}, u32[]{:S(2)}) copy-start(bf16[4,1536,128]{2,1,0:T(8,128)(2,1)S(1)} %concatenate.17.qf_ref) | copy-start | bytes 4718596
  75.2 6.4 %copy-start.3 = (bf16[512,1024]{1,0:T(8,128)(2,1)S(1)}, bf16[512,1024]{1,0:T(8,128)(2,1)}, u32[]{:S(2)}) copy-start(bf16[512,1024]{1,0:T(8,128)(2,1)} %down_w_ref.1) | copy-start | bytes 3145732
  75.2 6.4 %copy-start.4 = (bf16[128,4096]{1,0:T(8,128)(2,1)S(1)}, bf16[128,4096]{1,0:T(8,128)(2,1)}, u32[]{:S(2)}) copy-start(bf16[128,4096]{1,0:T(8,128)(2,1)} %in_w_ref.1) | copy-start | bytes 3145732
  75.2 6.4 %copy-start.5 = (bf16[128,1024]{1,0:T(8,128)(2,1)S(1)}, bf16[128,1024]{1,0:T(8,128)(2,1)}, u32[]{:S(2)}) copy-start(bf16[128,1024]{1,0:T(8,128)(2,1)} %out_w_ref.1) | copy-start | bytes 786436
  81.6 108.9 %copy-start.9 = (bf16[1,384,1024]{2,1,0:T(8,128)(2,1)S(1)}, bf16[1,384,1024]{2,1,0:T(8,128)(2,1)}, u32[]{:S(2)}) copy-start(bf16[1,384,1024]{2,1,0:T(8,128)(2,1)} %param.14) | copy-start | bytes 2359300
  190.5 1.5 copy-start.2
  190.5 1.5 copy-start.6
  190.5 2.1 copy-start.7
  190.5 2.4 copy-start.17
  190.5 2.4 copy-start.19
  192.6 21.0 %copy-start.11 = (f32[384,1024]{1,0:T(8,128)}, f32[384,1024]{1,0:T(8,128)S(1)}, u32[]{:S(2)}) copy-start(f32[384,1024]{1,0:T(8,128)S(1)} %get-tuple-element.89) | copy-start | bytes 4718596
  192.6 7.1 %slice-start.2 = ((s8[8388608]{0:T(1024)(128)(4,1)}), s8[4194304]{0:T(1024)(128)(4,1)S(1)}, s32[]{:S(2)}) async-start(s8[8388608]{0:T(1024)(128)(4,1)} %bitcast.137), calls=%async_computation.2 | async-start | bytes 8388608
  192.9 6.8 %copy-start.20 = (f32[1024]{0:T(1024)S(1)}, f32[1024]{0:T(1024)}, u32[]{:S(2)}) copy-start(f32[1024]{0:T(1024)} %get-tuple-element.77) | copy-start | bytes 12292
  192.9 6.8 %slice-start.3 = ((s8[8388608]{0:T(1024)(128)(4,1)}), s8[4194304]{0:T(1024)(128)(4,1)S(1)}, s32[]{:S(2)}) async-start(s8[8388608]{0:T(1024)(128)(4,1)} %bitcast.137), calls=%async_computation.3 | async-start | bytes 8388608
  199.8 4.9 %copy-start.23 = (f32[384,4096]{1,0:T(8,128)}, f32[384,4096]{1,0:T(8,128)S(1)}, u32[]{:S(2)}) copy-start(f32[384,4096]{1,0:T(8,128)S(1)} %convolution_add_fusion) | copy-start | bytes 18874372
  199.8 4.9 %copy-start.15 = (bf16[1,384,1024]{2,1,0:T(8,128)(2,1)S(1)}, bf16[1,384,1024]{2,1,0:T(8,128)(2,1)}, u32[]{:S(2)}) copy-start(bf16[1,384,1024]{2,1,0:T(8,128)(2,1)} %param.27) | copy-start | bytes 2359300
  199.8 13.8 %slice-start = ((s8[8388608]{0:T(1024)(128)(4,1)}), s8[4194304]{0:T(1024)(128)(4,1)S(1)}, s32[]{:S(2)}) async-start(s8[8388608]{0:T(1024)(128)(4,1)} %bitcast.135), calls=%async_computation | async-start | bytes 8388608
  204.7 9.0 %slice-start.1 = ((s8[8388608]{0:T(1024)(128)(4,1)}), s8[4194304]{0:T(1024)(128)(4,1)S(1)}, s32[]{:S(2)}) async-start(s8[8388608]{0:T(1024)(128)(4,1)} %bitcast.135), calls=%async_computation.1 | async-start | bytes 8388608
  213.6 4.9 %copy-start.21 = (bf16[384,4096]{1,0:T(8,128)(2,1)}, bf16[384,4096]{1,0:T(8,128)(2,1)S(1)}, u32[]{:S(2)}) copy-start(bf16[384,4096]{1,0:T(8,128)(2,1)S(1)} %get-tuple-element.93) | copy-start | bytes 9437188
  218.5 2.7 copy-start.8
  218.5 7.3 %slice-start.4 = ((s8[6291456]{0:T(1024)(128)(4,1)}), s8[4194304]{0:T(1024)(128)(4,1)S(1)}, s32[]{:S(2)}) async-start(s8[6291456]{0:T(1024)(128)(4,1)} %bitcast.139), calls=%async_computation.4 | async-start | bytes 8388608
  221.3 4.6 slice-start.5
  225.8 7.3 %copy-start.12 = (f32[384,1024]{1,0:T(8,128)S(1)}, f32[384,1024]{1,0:T(8,128)}, u32[]{:S(2)}) copy-start(f32[384,1024]{1,0:T(8,128)} %copy-done.11) | copy-start | bytes 4718596
  225.8 7.3 %copy-start.22 = (bf16[384,4096]{1,0:T(8,128)(2,1)S(1)}, bf16[384,4096]{1,0:T(8,128)(2,1)}, u32[]{:S(2)}) copy-start(bf16[384,4096]{1,0:T(8,128)(2,1)} %copy-done.21) | copy-start | bytes 9437188
  240.5 153.7 %copy-start.10 = (bf16[1,384,1024]{2,1,0:T(8,128)(2,1)S(1)}, bf16[1,384,1024]{2,1,0:T(8,128)(2,1)}, u32[]{:S(2)}) copy-start(bf16[1,384,1024]{2,1,0:T(8,128)(2,1)} %param.14) | copy-start | bytes 2359300
  400.5 1.6 copy-start.18
  456.2 2.7 copy-start.16
  459.7 3.3 copy-start.13
